TPU v7x, 32 devices: a whole 2x2x4 slice. The times are simulated.
32 devices in a mesh: rows: 2 (over x), gr: 4 (over z), gc: 4 (over y, core).
Axes of the slice: x: 2, y: 2, z: 4, core: 2. Of those that a mesh axis runs over, the one named last changes fastest.
Arguments:
- tokens: bfloat16 [32768, 768], P(('rows', 'gr', 'gc')), may hold values from -6 to 6
- boxes: int32 [4, 32768], P(None, ('rows', 'gr', 'gc')), may hold values from 0 to 1000
- page_ids: int32 [64, 512], P(('rows', 'gr', 'gc')), may hold values from 0 to 3, never falling along the last dimension, each value on 1 to 256 neighbouring positions
- seg_ids: int32 [64, 512], P(('rows', 'gr', 'gc')), may hold values from 0 to 63, never falling along the last dimension, each value on 1 to 24 neighbouring positions
- pair_mask: int32 [2, 2048, 2048], P('rows', 'gr', 'gc'), may hold values 0 or 1
- ln1_gain: float32 [768], replicated, may hold values from 0.5 to 1.5
- ln1_bias: float32 [768], replicated, may hold values from -3 to 3
- query_key_value_weight: bfloat16 [768, 2304], replicated, may hold values from -0.21875 to 0.21875
- attention_output_weight: bfloat16 [768, 768], replicated, may hold values from -0.625 to 0.625
- ln2_gain: float32 [768], replicated, may hold values from 0.5 to 1.5
- ln2_bias: float32 [768], replicated, may hold values from -3 to 3
- up_projection_weight: bfloat16 [768, 3072], replicated, may hold values from -0.21875 to 0.21875
- up_projection_bias: float32 [3072], replicated, may hold values from -3 to 3
- down_projection_weight: bfloat16 [3072, 768], replicated, may hold values from -0.15625 to 0.15625
- box_table: float32 [12, 128], replicated, may hold values from -3 to 3
- rel_left: bfloat16 [768, 768], replicated, may hold values from -0.21875 to 0.21875
- rel_right: bfloat16 [768, 768], replicated, may hold values from -0.21875 to 0.21875
- cot_out: bfloat16 [32768, 768], P(('rows', 'gr', 'gc')), may hold values from -6 to 6
- cot_logits: bfloat16 [2, 2048, 2048], P('rows', 'gr', 'gc'), may hold values from -6 to 6
Outputs:
- layer_out: bfloat16 [32768, 768], P(('rows', 'gr', 'gc'))
- pair_logits: float32 [2, 2048, 2048], P('rows', 'gr', 'gc')
- grad_tokens: float32 [32768, 768], P(('rows', 'gr', 'gc'))
- grad_ln1_gain: float32 [768], replicated
- grad_ln1_bias: float32 [768], replicated
- grad_qkv: float32 [1769472], P(('rows', 'gr', 'gc'))
- grad_out_weight: float32 [589824], P(('rows', 'gr', 'gc'))
- grad_ln2_gain: float32 [768], replicated
- grad_ln2_bias: float32 [768], replicated
- grad_up: float32 [2359296], P(('rows', 'gr', 'gc'))
- grad_up_bias: float32 [3072], replicated
- grad_down: float32 [2359296], P(('rows', 'gr', 'gc'))
- grad_box_table: float32 [12, 128], replicated
- grad_rel_left: float32 [589824], P(('rows', 'gr', 'gc'))
- grad_rel_right: float32 [589824], P(('rows', 'gr', 'gc'))
Inputs may be any that keep to these rules, and one draw needn't show every extreme that they name: `page_ids`: within a packed row page ids never fall; each of the 4 pages has 1 to 256 tokens. `seg_ids`: within a packed row segment slots never fall; each of the 64 slots has 1 to 24 tokens.
All inputs are finite; a program needn't handle non-finite values. No bound on the sum of `pair_mask` on one device may be relied on, other than what follows from the above.
Results may differ from a plain program's by a relative error of at most 0.03.
Values may be sent and summed in bfloat16 or wider, within the bound.
A program may use at most 192 MiB of HBM per device.

v0:
```python
import functools
import math

import jax
import jax.numpy as jnp
from jax import lax
from jax.experimental import pallas as pl
from jax.experimental.pallas import tpu as pltpu
from jax.sharding import PartitionSpec as P

COORD=1000
SPAN=2*COORD+1
LOG2E=1.4426950408889634
BARRED=-2.0**99
SLOTS=64
BF=jnp.bfloat16
F32=jnp.float32
NT=(((1,),(1,)),((),()))
NN=(((1,),(0,)),((),()))
def dot(a,b,dims=NN):
    return lax.dot_general(a,b,dims,preferred_element_type=F32)

def whole_and_rest(scaled):
    whole=jnp.floor((scaled+0.5)*(1.0/SPAN))
    return whole, scaled-SPAN*whole

def key_side(low, high, half):
    c=jnp.floor((low+high).astype(F32)*0.5)
    return whole_and_rest(c*half)
def query_side(low, high, half):
    c=jnp.floor((low+high).astype(F32)*0.5)
    return whole_and_rest((COORD-c)*half)

def hi_lo(v):
    hi=v.astype(BF)
    return hi, (v-hi.astype(F32)).astype(BF)

def fwd_kernel(q_ref,k_ref,v_ref,boxr_ref,boxc_ref,tab_ref,mask_ref,cot_ref,
               ctx_ref,e_ref,linv_ref,rowp_ref,colp_ref,
               ohb_ref,oha_ref,kg_ref,rxy_ref,pg_ref,cx_ref,cy_ref,*panel_refs,rows,pair_scale):
    length=q_ref.shape[0]
    half=tab_ref.shape[1]//2
    quarter=half//2
    hp=pl.program_id(1)
    seq=pl.program_id(0)
    place=Place(1)
    mask_buf,cot_buf,in_sem=panel_refs[:3]
    panels=Panels(place,*panel_refs[3:7],panel_refs[7:])
    def inputs():
        return (pltpu.make_async_copy(mask_ref,mask_buf,in_sem.at[0]),
                pltpu.make_async_copy(cot_ref,cot_buf,in_sem.at[1]))
    @pl.when((hp==0)&(seq==0))
    def _():
        for copy in inputs():
            copy.start()
    @pl.when((hp==1)&(seq==0))
    def _():
        for copy in inputs():
            copy.wait()
        panels.fill(mask_buf,cot_buf,pair_scale)
        meet([place.gc_peer(d) for d in (1,2,3)]+[place.gr_peer(d) for d in (1,2,3)])
    @pl.when((hp==2)&(seq==0))
    def _():
        panels.start()
    lane=lax.broadcasted_iota(jnp.int32,(1,128),1)
    low=lane<64
    @pl.when(hp==0)
    def _():
        bc=boxc_ref[...]
        ax,fax=key_side(bc[:,0:1],bc[:,2:3],half)
        ay,fay=key_side(bc[:,1:2],bc[:,3:4],half)
        bx,fbx=query_side(bc[:,0:1],bc[:,2:3],half)
        by,fby=query_side(bc[:,1:2],bc[:,3:4],half)
        spot=(lane%quarter).astype(F32)
        is_x=(lane%half)<quarter
        oha=jnp.where(jnp.where(is_x,ax,ay)==spot,1.0,0.0)
        ohb=jnp.where(jnp.where(is_x,bx,by)==(quarter-1)-spot,1.0,0.0)
        ohb_ref[...]=jnp.where(low,ohb,0.0).astype(BF)
        oha_ref[...]=oha.astype(BF)
        page=bc[:,4:5].astype(jnp.int32)
        mine=(lane%64)==page
        barred=jnp.where((lane%64)<4,jnp.where(mine,0.0,BARRED),0.0)
        kg_ref[0]=jnp.where(low,oha,barred).astype(BF)
        kg_ref[1]=jnp.where(low,barred,oha).astype(BF)
        pg_ref[...]=jnp.where(mine,1.0,0.0).astype(BF)
        ohx=jnp.where(ax==spot,1.0,0.0)
        ohy=jnp.where(ay==spot,1.0,0.0)
        rxy_ref[pl.ds(0,length),:]=jnp.where(low,ohx,0.0).astype(BF)
        rxy_ref[pl.ds(length,length),:]=jnp.where(low,0.0,ohy).astype(BF)
        br=boxr_ref[...]
        _,gax=key_side(br[0:1],br[2:3],half)
        _,gay=key_side(br[1:2],br[3:4],half)
        cx_ref[...]=jnp.where(gax+fbx>=SPAN,1.0,0.0)
        cy_ref[...]=jnp.where(gay+fby>=SPAN,1.0,0.0)
    k=k_ref[...]
    v=v_ref[...]
    oha=oha_ref[...]
    b_row=lax.broadcasted_iota(jnp.int32,(half,128),0)
    l_col=lax.broadcasted_iota(jnp.int32,(half,128),1)
    row_x=b_row<quarter
    same_axis=row_x==((l_col%half)<quarter)
    d_axis=row_x==(l_col<half)
    heads=[]
    for a in range(2):
        t=tab_ref[pl.ds(2*hp+a,1),:]
        both=[jnp.where(low,t,0.0)+pltpu.roll(jnp.where(low,t,0.0),64,1),
              jnp.where(low,0.0,t)+pltpu.roll(jnp.where(low,0.0,t),64,1)]
        tiles=[]
        for b in both:
            spreads=[]
            for first in (0,1):
                whole=jnp.broadcast_to(b,(quarter,128))
                turned=pltpu.roll(whole,128-(quarter-1)-first,1,stride=1,stride_axis=0)
                lowq=jnp.where(lane<quarter,turned,0.0)
                pair=lowq+pltpu.roll(lowq,quarter,1)
                spreads.append(pair+pltpu.roll(pair,64,1))
            tiles.append(spreads)
        base=jnp.concatenate([tiles[0][0],tiles[1][0]],axis=0)
        nxt=jnp.concatenate([tiles[0][1],tiles[1][1]],axis=0)
        hi,lo=hi_lo(base)
        dhi,dlo=hi_lo(nxt-base)
        z=jnp.zeros_like(hi)
        is_hi=(l_col<64)==(a==1)
        g0=jnp.where(same_axis,jnp.where(is_hi,hi.astype(F32),lo.astype(F32)),0.0).astype(BF)
        g1=jnp.where(d_axis,jnp.where((l_col%half)<quarter,dhi.astype(F32),dlo.astype(F32)),0.0).astype(BF)
        hk=jnp.concatenate([g0,g1],axis=1)
        left=dot(ohb_ref[:,0:half],hk).astype(BF)
        if a==0:
            rhs=jnp.concatenate([jnp.where(low,k,oha),kg_ref[0]],axis=1)
            vv=jnp.where(low,v,jnp.ones_like(v))
        else:
            rhs=jnp.concatenate([jnp.where(low,oha,k),kg_ref[1]],axis=1)
            vv=jnp.where(low,jnp.ones_like(v),v)
        heads.append((left,rhs,vv))
    for c in range(length//rows):
        sl=pl.ds(c*rows,rows)
        q=q_ref[sl,:]*jnp.asarray(0.125,BF)
        pg=pg_ref[sl,:]
        outs=[]
        for a in range(2):
            left,rhs,vv=heads[a]
            lc=left[c*rows:(c+1)*rows]
            g0=lc[:,:128]
            if a==0:
                lhs=jnp.concatenate([jnp.where(low,q,g0),jnp.where(low,g0,pg)],axis=1)
            else:
                lhs=jnp.concatenate([jnp.where(low,g0,q),jnp.where(low,pg,g0)],axis=1)
            s=dot(lhs,rhs,NT)
            dxy=dot(lc[:,128:],rxy_ref[...],NT)
            s=s+cx_ref[sl,:]*dxy[:,:length]+cy_ref[sl,:]*dxy[:,length:]
            m=jnp.max(s,axis=1,keepdims=True)
            e=jnp.exp2((s-m)*LOG2E).astype(BF)
            e_ref[a,sl,:]=e
            outs.append(dot(e,vv))
        ctx=jnp.where(low,outs[0],outs[1])
        tot=jnp.where(low,pltpu.roll(outs[0],64,1),pltpu.roll(outs[1],64,1))
        linv=1.0/tot
        linv_ref[sl,:]=linv
        ctx_ref[sl,:]=(ctx*linv).astype(BF)
    @pl.when((hp==pl.num_programs(1)-1)&(seq==pl.num_programs(0)-1))
    def _():
        panels.collect(rowp_ref,colp_ref)

def attend_forward(qkv,boxes_r,boxes_c,seqs,table,mask,cot,pair_scale,rows=512):
    tokens,width=qkv.shape
    feats=width//3
    length=tokens//seqs
    heads=table.shape[0]
    pairs=heads//2
    return pl.pallas_call(
        functools.partial(fwd_kernel,rows=rows,pair_scale=pair_scale),
        grid=(seqs,pairs),
        in_specs=[
            pl.BlockSpec((length,128),lambda s,h:(s,h)),
            pl.BlockSpec((length,128),lambda s,h:(s,pairs+h)),
            pl.BlockSpec((length,128),lambda s,h:(s,2*pairs+h)),
            pl.BlockSpec((4,length),lambda s,h:(0,s)),
            pl.BlockSpec((length,128),lambda s,h:(s,0)),
            pl.BlockSpec(table.shape,lambda s,h:(0,0)),
            pl.BlockSpec(memory_space=pl.ANY),
            pl.BlockSpec(memory_space=pl.ANY),
        ],
        out_specs=[
            pl.BlockSpec((length,128),lambda s,h:(s,h)),
            pl.BlockSpec((2,None,length,length),lambda s,h:(h,s,0,0)),
            pl.BlockSpec((length,128),lambda s,h:(s,h)),
            pl.BlockSpec(memory_space=pltpu.VMEM),
            pl.BlockSpec(memory_space=pltpu.VMEM),
        ],
        out_shape=[jax.ShapeDtypeStruct((tokens,feats),BF),
                   jax.ShapeDtypeStruct((heads,seqs,length,length),BF),
                   jax.ShapeDtypeStruct((tokens,feats),F32)]
                  +[jax.ShapeDtypeStruct((4,mask.shape[0]//4,mask.shape[0]),BF)]*2,
        scratch_shapes=[pltpu.VMEM((length,128),BF),pltpu.VMEM((length,128),BF),
                        pltpu.VMEM((2,length,128),BF),pltpu.VMEM((2*length,128),BF),
                        pltpu.VMEM((length,128),BF),
                        pltpu.VMEM((length,length),F32),pltpu.VMEM((length,length),F32)]
                       +[pltpu.VMEM(mask.shape,jnp.int32),pltpu.VMEM(cot.shape,BF),pltpu.SemaphoreType.DMA((2,))]
                       +Panels.scratch(mask.shape[0]),
        compiler_params=pltpu.CompilerParams(collective_id=4,has_side_effects=True,vmem_limit_bytes=60<<20),
        name="attend_forward",
    )(qkv,qkv,qkv,boxes_r,boxes_c,table,mask,cot)


AXES = ("rows", "gr", "gc")
MESH = pl.DeviceIdType.MESH
PIECE = 384


class Place:
    def __init__(self, n_rows):
        self.n_rows = n_rows
        self.r = lax.axis_index("rows")
        self.g = lax.axis_index("gr")
        self.c = lax.axis_index("gc")
        self.core = lax.rem(self.c, 2)
        self.u = lax.div(self.c, 2)
        self.sibling = {"gc": self.u * 2 + 1 - self.core}
        self.across = {"gc": (1 - self.u) * 2 + self.core}

    def row_peer(self, d):
        return {"rows": lax.rem(self.r + d, self.n_rows)}

    def gr_peer(self, d):
        return {"gr": lax.rem(self.g + d, 4)}

    def gc_peer(self, d):
        return {"gc": lax.rem(self.c + d, 4)}

    def peers(self):
        return (
            [self.sibling, self.across]
            + [self.row_peer(d) for d in range(1, self.n_rows)]
            + [self.gr_peer(d) for d in range(1, 4)]
        )


def meet(peers):
    barrier = pltpu.get_barrier_semaphore()
    for peer in peers:
        pl.semaphore_signal(barrier, inc=1, device_id=peer, device_id_type=MESH)
    pl.semaphore_wait(barrier, len(peers))


def send(src, dst, send_sem, recv_sem, peer):
    return pltpu.make_async_remote_copy(
        src_ref=src, dst_ref=dst, send_sem=send_sem, recv_sem=recv_sem, device_id=peer,
        device_id_type=MESH,
    )


def by_step(step, first, end, action):
    if end - first == 1:
        action(first)
        return
    middle = (first + end) // 2
    pl.when(step < middle)(lambda: by_step(step, first, middle, action))
    pl.when(step >= middle)(lambda: by_step(step, middle, end, action))


class Unit:
    def __init__(self, array, part, block, rows_first, beats, source=None, leave=None):
        self.array, self.part, self.block = array, part, block
        self.rows_first, self.beats, self.source, self.leave = rows_first, beats, source, leave
        self.stages = sorted(stage for stage in beats if stage != "in")
        self.fresh = self.stages[0] == 0

    def does(self, stage):
        return stage in self.beats


class Shares:
    def __init__(self, place, units, piece, arrays, staging, carried, fins, got, bufs, sems, ends):
        self.p = place
        self.units = units
        self.piece = piece
        self.arrays = arrays
        self.staging = staging
        self.carried = carried
        self.fin = fins
        self.got = got
        self.own, self.b0, self.b1r, self.b1u, self.b2r, self.b2u, self.b3 = bufs
        self.ls, self.ss, self.rs = sems
        self.fs, self.fr = ends
        external = [i for i, unit in enumerate(units) if unit.source is None]
        self.external = sorted(external, key=lambda i: units[i].beats[0])

    def number(self, i, test):
        return sum(test(unit) for unit in self.units[:i])

    @staticmethod
    def kinds():
        return (
            lambda unit: True,
            lambda unit: unit.does(0),
            lambda unit: unit.does(1) and unit.rows_first,
            lambda unit: unit.does(1) and not unit.rows_first,
            lambda unit: unit.does(2) and not unit.rows_first,
            lambda unit: unit.does(2) and unit.rows_first,
            lambda unit: unit.does(3),
        )

    @staticmethod
    def scratch(units, piece, n_rows):
        n, m, r = len(units), 48, n_rows
        shapes = (
            (r, 4, 2, m), (r, 4, 2, m), (r - 1, 4, 2, m), (r, 4, m), (r - 1, 4, m), (4, m), (3, m),
        )
        bufs = [
            pltpu.VMEM((max(1, sum(map(test, units))),) + shape + (piece,), BF)
            for test, shape in zip(Shares.kinds(), shapes)
        ]
        dma = pltpu.SemaphoreType.DMA
        return bufs + [dma((n,)), dma((n, r + 4)), dma((n, r + 4))]

    @staticmethod
    def result_scratch(sizes):
        dma = pltpu.SemaphoreType.DMA
        k = len(sizes)
        fins = [pltpu.VMEM((2, rows, x // 2), F32) for rows, x in sizes]
        got = [pltpu.VMEM((rows, x // 2), F32) for rows, x in sizes]
        return fins + got + [dma((k,)), dma((k,))]

    def buffer(self, kind, i):
        bufs = (self.own, self.b0, self.b1r, self.b1u, self.b2r, self.b2u, self.b3)
        return bufs[kind].at[self.number(i, self.kinds()[kind])]

    def piece_of(self, i, core):
        unit = self.units[i]
        if unit.source is None:
            at = unit.block * 2 * self.piece + core * self.piece
            columns = pl.ds(pl.multiple_of(at, 128), self.piece)
            return self.arrays[unit.array].at[:, :, :, unit.part, :, columns]
        _, n, column = unit.source
        return self.staging.at[n, core, :, :, :, :, column : column + self.piece]

    def swap(self, i):
        src = self.piece_of(i, 1 - self.p.core)
        return send(src, self.buffer(1, i), self.ss.at[i, 0], self.rs.at[i, 0], self.p.sibling)

    def keep(self, i):
        unit, p = self.units[i], self.p
        if unit.source is None:
            src, to = self.piece_of(i, p.core), self.own.at[i]
        else:
            src = self.carried[unit.source[1]].at[unit.source[2]]
            if unit.does(2):
                to = self.own.at[i, p.r] if unit.rows_first else self.own.at[i, :, :, p.u]
            else:
                to = self.own.at[i, p.r, :, p.u]
        return pltpu.make_async_copy(src, to, self.ls.at[i])

    def along_rows(self, i, first):
        p = self.p
        out = []
        for d in range(1, p.n_rows):
            to = lax.rem(p.r + d, p.n_rows)
            src = self.own.at[i, to] if first else self.own.at[i, to, :, p.u]
            dst = self.buffer(2 if first else 4, i).at[d - 1]
            out.append(send(src, dst, self.ss.at[i, 1 + d], self.rs.at[i, 1 + d], p.row_peer(d)))
        return out

    def across(self, i, first):
        p = self.p
        src = self.own.at[i, :, :, 1 - p.u] if first else self.own.at[i, p.r, :, 1 - p.u]
        dst = self.buffer(3 if first else 5, i)
        return [send(src, dst, self.ss.at[i, 1], self.rs.at[i, 1], p.across)]

    def along_gr(self, i):
        p = self.p
        out = []
        for d in range(1, 4):
            src = self.own.at[i, p.r, lax.rem(p.g + d, 4), p.u]
            at = p.n_rows + d
            dst = self.buffer(6, i).at[d - 1]
            out.append(send(src, dst, self.ss.at[i, at], self.rs.at[i, at], p.gr_peer(d)))
        return out

    def copies(self, i, stage):
        if stage == 0:
            return [self.swap(i)]
        if stage == 3:
            return self.along_gr(i)
        if self.units[i].rows_first == (stage == 1):
            return self.along_rows(i, stage == 1)
        return self.across(i, stage == 1)

    def start(self, i, stage):
        if stage == 0 and self.units[i].source is None:
            self.keep(i).start()
        for copy in self.copies(i, stage):
            copy.start()

    def finish(self, i, stage):
        p, unit = self.p, self.units[i]
        if stage == 0 and unit.source is None:
            self.keep(i).wait()
        for copy in self.copies(i, stage):
            copy.wait_recv()
        if stage == 0:
            to = self.own.at[i]
            mine = to if unit.source is None else self.piece_of(i, p.core)
            theirs = self.buffer(1, i)

            @pl.loop(0, 4)
            def _(n):
                to[:, n] = mine[:, n] + theirs[:, n]

            return
        if stage == 3:
            total = self.own[i, p.r, p.g, p.u].astype(F32)
            for d in range(3):
                total = total + self.buffer(6, i)[d].astype(F32)
            m = total.shape[0]
            fin = self.fin[unit.array]
            rows = fin.shape[1]
            span = slice(unit.block * self.piece, (unit.block + 1) * self.piece)
            if rows < m:
                fin[0, :, span] = total[:rows]
                fin[1, :, span] = total[rows:]
            else:
                per = rows // m
                row = (unit.part % per) * m
                fin[unit.part // per, row : row + m, span] = total
            return
        if stage == 2:
            to = self.own.at[i, p.r, :, p.u]
        else:
            to = self.own.at[i, p.r] if unit.rows_first else self.own.at[i, :, :, p.u]
        if unit.rows_first == (stage == 1):
            terms = [self.buffer(2 if stage == 1 else 4, i).at[d] for d in range(p.n_rows - 1)]
        else:
            terms = [self.buffer(3 if stage == 1 else 5, i)]
        out = to
        if unit.leave is not None and stage == unit.stages[-1]:
            out = self.carried[unit.leave[0]].at[unit.leave[1]]
        if stage == 1:
            @pl.loop(0, 4)
            def _(n):
                at = n if unit.rows_first else (slice(None), n)
                total = to[at]
                for term in terms:
                    total = total + term[at]
                out[at] = total
        else:
            total = to[...]
            for term in terms:
                total = total + term[...]
            out[...] = total

    def last(self, k):
        return send(
            self.fin[k].at[1 - self.p.core], self.got[k], self.fs.at[k], self.fr.at[k],
            self.p.sibling,
        )

    def begin(self, window):
        for i, unit in enumerate(self.units):
            if not unit.fresh:
                self.keep(i).start()
        for i in self.external[:window]:
            self.start(i, 0)

    def tick(self, t, window, done):
        due = []
        for i, unit in enumerate(self.units):
            for stage, beat in unit.beats.items():
                if beat == t:
                    due.append((-1 if stage == "in" else stage, i))
        for stage, i in sorted(due, key=lambda entry: (-entry[0], entry[1])):
            unit = self.units[i]
            if stage < 0:
                self.keep(i).wait()
                self.start(i, unit.stages[0])
                continue
            self.finish(i, stage)
            if stage == 0 and i in self.external:
                later = self.external.index(i) + window
                if later < len(self.external):
                    self.start(self.external[later], 0)
            if stage == 3:
                final, count = done[unit.array]
                if t == final:
                    done[unit.array] = final, count - 1
                    if count == 1:
                        self.last(unit.array).start()
            elif stage < unit.stages[-1]:
                self.start(i, stage + 1)

    def ticks(self):
        return 1 + max(beat for unit in self.units for beat in unit.beats.values())

    def deliver(self, k, out, spans):
        core = self.p.core
        self.last(k).wait()
        for value, owner in ((self.fin[k][core], core), (self.got[k][...], 1 - core)):
            at = 0
            for base, step, width in spans:
                where = pl.ds(pl.multiple_of(base + owner * step, 128), width)
                out[:, where] = value[:, at : at + width]
                at += width

    def wait_sends(self):
        for i, unit in enumerate(self.units):
            for stage in unit.stages:
                for copy in self.copies(i, stage):
                    copy.wait_send()


def on_the_way(units, arrays):
    beats = [[unit.beats[3] for unit in units if unit.array == k and unit.does(3)] for k in range(arrays)]
    return [(max(of), of.count(max(of))) if of else (-1, 0) for of in beats]


class Total:
    def __init__(self, place, source, out, bufs, sems):
        self.p = place
        self.src = source
        self.out = out
        self.part, self.pair, self.high, self.rows, self.quad = bufs
        self.ss, self.rs = sems

    @staticmethod
    def scratch(shape, n_rows):
        dma = pltpu.SemaphoreType.DMA
        bufs = [
            pltpu.VMEM((3,) + shape, F32), pltpu.VMEM(shape, F32), pltpu.VMEM(shape, F32),
            pltpu.VMEM((n_rows,) + shape, F32), pltpu.VMEM((4,) + shape, F32),
        ]
        return bufs, [dma((n_rows + 4,)), dma((n_rows + 4,))]

    def copies(self, stage):
        p = self.p
        if stage == 0:
            return [send(self.src, self.pair, self.ss.at[0], self.rs.at[0], p.sibling)]
        if stage == 1:
            return [send(self.part.at[0], self.high, self.ss.at[1], self.rs.at[1], p.across)]
        if stage == 2:
            return [
                send(
                    self.part.at[1], self.rows.at[p.r], self.ss.at[1 + d], self.rs.at[1 + d],
                    p.row_peer(d),
                )
                for d in range(1, p.n_rows)
            ]
        return [
            send(
                self.part.at[2], self.quad.at[p.g], self.ss.at[p.n_rows + d],
                self.rs.at[p.n_rows + d], p.gr_peer(d),
            )
            for d in range(1, 4)
        ]

    def start(self, stage):
        for copy in self.copies(stage):
            copy.start()

    def finish(self, stage):
        p = self.p
        for copy in self.copies(stage):
            copy.wait_recv()
        if stage == 0:
            self.part[0] = self.src[...] + self.pair[...]
        elif stage == 1:
            self.part[1] = self.part[0] + self.high[...]
        elif stage == 2:
            self.rows[p.r] = self.part[1]
            total = self.rows[0]
            for d in range(1, p.n_rows):
                total = total + self.rows[d]
            self.part[2] = total
        else:
            self.quad[p.g] = self.part[2]
            self.out[...] = (self.quad[0] + self.quad[1]) + (self.quad[2] + self.quad[3])

    def wait_sends(self):
        for stage in range(4):
            for copy in self.copies(stage):
                copy.wait_send()


def view(g, n_rows):
    rows, x = g.shape
    per = rows // (n_rows * 8)
    return g.reshape(n_rows, 4, 2, per // 48, 48, x)


def project_kernel(x_ref, gain_ref, bias_ref, w_ref, box_ref, page_ref, h1_ref, qkv_ref, cols_ref):
    @pl.when(pl.program_id(0) == 0)
    def _():
        chunk = 256
        count = x_ref.shape[0]

        @pl.loop(0, count // chunk)
        def _(c):
            sl = pl.ds(pl.multiple_of(c * chunk, chunk), chunk)
            x = x_ref[sl, :].astype(F32)
            average, inverse = norm_stats(x)
            h1_ref[sl, :] = ((x - average) * inverse * gain_ref[...].reshape(1, -1) + bias_ref[...].reshape(1, -1)).astype(BF)
        pages = jnp.concatenate([page_ref[s : s + 1, :] for s in range(page_ref.shape[0])], axis=1)
        lines = jnp.concatenate(
            [box_ref[...].astype(F32), pages.astype(F32), jnp.zeros((123, count), F32)], axis=0
        )
        cols_ref[...] = lines.T

    qkv_ref[...] = dot(h1_ref[...], w_ref[...]).astype(BF)


def project_forward(tokens, gain, bias, weight, boxes, page_ids):
    count, feats = tokens.shape
    width = weight.shape[1]
    block = 384
    vm = pl.BlockSpec(memory_space=pltpu.VMEM)
    return pl.pallas_call(
        project_kernel,
        grid=(width // block,),
        in_specs=[
            pl.BlockSpec((count, feats), lambda j: (0, 0)), vm, vm,
            pl.BlockSpec((feats, block), lambda j: (0, j)), vm, vm,
        ],
        out_specs=[vm, pl.BlockSpec((count, block), lambda j: (0, j)), vm],
        out_shape=[
            jax.ShapeDtypeStruct((count, feats), BF), jax.ShapeDtypeStruct((count, width), BF),
            jax.ShapeDtypeStruct((count, 128), F32),
        ],
        compiler_params=pltpu.CompilerParams(vmem_limit_bytes=63 << 20),
        name="project_forward",
    )(tokens, gain, bias, weight, boxes, page_ids)


def slot_members(seg_row, slots):
    ids = lax.broadcasted_iota(jnp.int32, (slots, seg_row.shape[1]), 0)
    return jnp.where(ids == seg_row, 1.0, 0.0)


def mlp_forward_kernel(
    ctx_ref, wo_ref, x_ref, gain_ref, bias_ref, wu_ref, bu_ref, wd_ref, seg_ref,
    r1_ref, h2_ref, act_ref, slope_ref, out_ref, emb_ref, acc_ref,
):
    step = pl.program_id(0)
    count = x_ref.shape[0]
    chunk = 256

    @pl.when(step == 0)
    def _():
        @pl.loop(0, count // chunk)
        def _(c):
            sl = pl.ds(pl.multiple_of(c * chunk, chunk), chunk)
            r1 = x_ref[sl, :].astype(F32) + dot(ctx_ref[sl, :], wo_ref[...])
            average, inverse = norm_stats(r1)
            r1_ref[sl, :] = r1
            acc_ref[sl, :] = r1
            h2_ref[sl, :] = ((r1 - average) * inverse * gain_ref[...].reshape(1, -1) + bias_ref[...].reshape(1, -1)).astype(BF)

    for c in range(count // chunk):
        sl = slice(c * chunk, (c + 1) * chunk)
        act, slope = gelu_pair(dot(h2_ref[sl, :], wu_ref[...]) + bu_ref[...])
        act = act.astype(BF)
        act_ref[sl, :] = act
        slope_ref[sl, :] = slope.astype(BF)
        acc_ref[sl, :] += dot(act, wd_ref[...])

    @pl.when(step == pl.num_programs(0) - 1)
    def _():
        out_ref[...] = acc_ref[...].astype(BF)
        seqs, length = seg_ref.shape
        slots = emb_ref.shape[0] // seqs
        for s in range(seqs):
            members = slot_members(seg_ref[s : s + 1, :], slots)
            total = dot(members.astype(BF), out_ref[s * length : (s + 1) * length, :])
            sizes = jnp.sum(members, axis=1, keepdims=True)
            emb_ref[s * slots : (s + 1) * slots, :] = (total / sizes).astype(BF)


def mlp_forward(ctx, w_out, tokens, gain, bias, w_up, b_up, w_down, seg_ids, slots):
    count, feats = tokens.shape
    hidden = w_up.shape[1]
    vm = pl.BlockSpec(memory_space=pltpu.VMEM)
    return pl.pallas_call(
        mlp_forward_kernel,
        grid=(hidden // feats,),
        in_specs=[
            vm, vm, vm, vm, vm, pl.BlockSpec((feats, feats), lambda f: (0, f)),
            pl.BlockSpec((1, feats), lambda f: (0, f)), pl.BlockSpec((feats, feats), lambda f: (f, 0)), vm,
        ],
        out_specs=[
            vm, vm, pl.BlockSpec((count, feats), lambda f: (0, f)),
            pl.BlockSpec((count, feats), lambda f: (0, f)), vm, vm,
        ],
        out_shape=[
            jax.ShapeDtypeStruct((count, feats), F32), jax.ShapeDtypeStruct((count, feats), BF),
            jax.ShapeDtypeStruct((count, hidden), BF), jax.ShapeDtypeStruct((count, hidden), BF),
            jax.ShapeDtypeStruct((count, feats), BF),
            jax.ShapeDtypeStruct((seg_ids.shape[0] * slots, feats), BF),
        ],
        scratch_shapes=[pltpu.VMEM((count, feats), F32)],
        compiler_params=pltpu.CompilerParams(vmem_limit_bytes=50 << 20),
        name="mlp_forward",
    )(
        ctx, w_out, tokens, gain, bias, w_up,
        b_up.reshape(1, hidden), w_down, seg_ids,
    )


class Panels:
    def __init__(self, place, tile, tile_t, rows, cols, sems):
        self.p = place
        self.tile, self.tile_t, self.rows, self.cols = tile, tile_t, rows, cols
        self.ss, self.rs = sems

    @staticmethod
    def scratch(size):
        dma = pltpu.SemaphoreType.DMA
        part = size // 4
        return [
            pltpu.VMEM((4, part, size), BF), pltpu.VMEM((4, part, size), BF),
            pltpu.VMEM((3, part, size), BF), pltpu.VMEM((3, part, size), BF), dma((6,)), dma((6,)),
        ]

    def copies(self):
        p = self.p
        out = []
        for d in range(1, 4):
            for n, (src, dst, peer, at) in enumerate((
                (self.tile, self.rows, p.gc_peer(d), p.c), (self.tile_t, self.cols, p.gr_peer(d), p.g),
            )):
                at_sem = 3 * n + d - 1
                out.append(
                    send(
                        src.at[lax.rem(at + d, 4)], dst.at[d - 1], self.ss.at[at_sem],
                        self.rs.at[at_sem], peer,
                    )
                )
        return out

    def fill(self, mask, cot, scale):
        g_raw = cot[...].astype(F32) * scale * mask[...].astype(F32)
        self.tile[...] = g_raw.astype(BF).reshape(self.tile.shape)
        self.tile_t[...] = g_raw.T.astype(BF).reshape(self.tile_t.shape)

    def start(self):
        for copy in self.copies():
            copy.start()

    def collect(self, row_out, col_out):
        p = self.p
        for copy in self.copies():
            copy.wait()
        row_out[p.c] = self.tile[p.c]
        col_out[p.g] = self.tile_t[p.g]
        for d in range(1, 4):
            row_out[lax.rem(p.c + 4 - d, 4)] = self.rows[d - 1]
            col_out[lax.rem(p.g + 4 - d, 4)] = self.cols[d - 1]


class Spread:
    def __init__(self, place, blocks, sems):
        self.p = place
        self.e = blocks
        self.ss, self.rs = sems
        self.near = lax.rem(place.c + 2, 4)

    @staticmethod
    def scratch(shape):
        dma = pltpu.SemaphoreType.DMA
        return [pltpu.VMEM((4, 4) + shape, BF), dma((4, 4, 3)), dma((4, 4))]

    def hop(self, row, col, kind, peer):
        block = self.e.at[row, col]
        return send(block, block, self.ss.at[row, col, kind], self.rs.at[row, col], peer)

    def own(self, step, waiting):
        p = self.p
        for sign in (1, -1) if step else (0,):
            row = p.g + sign * step
            inside = (row >= 0) & (row <= 3)

            @pl.when(inside)
            def _(row=row, sign=sign):
                if step and not waiting:
                    self.hop(row, p.c, 0, p.sibling).wait_recv()
                go = "wait_send" if waiting else "start"
                getattr(self.hop(row, p.c, 0, p.sibling), go)()
                getattr(self.hop(row, p.c, 1, p.across), go)()
                for way in (1, -1) if step == 0 else (-sign,):
                    to = p.g + way

                    @pl.when((to >= 0) & (to <= 3))
                    def _(to=to, way=way):
                        if step == 0 and way == -1:
                            copy = send(
                                self.e.at[row, p.c], self.e.at[row, p.c], self.down.at[0],
                                self.rs.at[row, p.c], {"gr": to},
                            )
                        else:
                            copy = self.hop(row, p.c, 2, {"gr": to})
                        getattr(copy, go)()

    def relay(self, step, waiting):
        p = self.p
        for sign in (1, -1) if step else (0,):
            row = p.g + sign * step

            @pl.when((row >= 0) & (row <= 3))
            def _(row=row):
                copy = self.hop(row, self.near, 0, p.sibling)
                if waiting:
                    copy.wait_send()
                else:
                    copy.wait_recv()
                    copy.start()

    def arrive(self, rows, cols):
        for row in rows:
            for col in cols:
                self.hop(row, col, 0, self.p.sibling).wait_recv()


def pair_kernel(
    emb_ref, left_ref, right_ref, rowp_ref, colp_ref, mask_ref, cot_ref, seg_ref,
    logits_ref, gleft_ref, gright_ref, gy_ref, gmlp_ref, e_ref, ss, rs, down, *, scale,
):
    place = Place(1)
    meet([place.sibling, place.across] + [place.gr_peer(d) for d in (1, 2, 3)])
    spread = Spread(place, e_ref, (ss, rs))
    spread.down = down
    p = place
    e_ref[p.g, p.c] = emb_ref[...]
    part, width = emb_ref.shape
    spread.own(0, False)
    spread.own(1, False)
    spread.relay(0, False)
    sib = p.u * 2 + 1 - p.core
    far = (1 - p.u) * 2 + 1 - p.core
    spread.arrive([p.g], [sib, far])
    left_rows = dot(e_ref[p.g].reshape(4 * part, width), left_ref[...]).astype(BF)
    spread.own(2, False)
    spread.relay(1, False)
    spread.own(3, False)
    right_cols = dot(e_ref[:, p.c].reshape(4 * part, width), right_ref[...]).astype(BF)
    spread.relay(2, False)
    logits_ref[...] = mask_ref[...].astype(F32) * dot(left_rows, right_cols, NT) * scale
    spread.relay(3, False)
    for d in range(1, 4):
        spread.arrive([lax.rem(p.g + d, 4)], [sib, far])
    row_sum = jnp.zeros((part, width), F32)
    col_sum = jnp.zeros((part, width), F32)
    for n in range(4):
        row_sum = row_sum + dot(rowp_ref[n], e_ref[:, n].reshape(4 * part, width))
        col_sum = col_sum + dot(colp_ref[n], e_ref[n].reshape(4 * part, width))

    def through(total, weight):
        high, low = hi_lo(total)
        return (dot(high, weight) + dot(low, weight)).astype(BF)

    g_left = through(row_sum, right_ref[...])
    g_right = through(col_sum, left_ref[...])
    emb_t = emb_ref[...].astype(F32).T.astype(BF)
    gleft_ref[...] = dot(emb_t, g_left).astype(BF)
    gright_ref[...] = dot(emb_t, g_right).astype(BF)
    g_emb = dot(g_left, left_ref[...], NT) + dot(g_right, right_ref[...], NT)
    seqs, length = seg_ref.shape
    slots = part // seqs
    for n in range(seqs):
        members = slot_members(seg_ref[n : n + 1, :], slots)
        g_seg = g_emb[n * slots : (n + 1) * slots] / jnp.sum(members, axis=1, keepdims=True)
        high, low = hi_lo(g_seg)
        twice = jnp.concatenate([members, members], axis=0).T.astype(BF)
        sl = slice(n * length, (n + 1) * length)
        g_y = cot_ref[sl, :].astype(F32) + dot(twice, jnp.concatenate([high, low], axis=0))
        gy_ref[sl, :] = g_y
        gmlp_ref[sl, :] = g_y.astype(BF)
    for step in range(4):
        spread.own(step, True)
        spread.relay(step, True)


def pair_head(emb, rel_left, rel_right, row_panel, col_panel, mask, cot_out, seg_ids, scale):
    part, width = emb.shape
    size = mask.shape[0]
    vm = pl.BlockSpec(memory_space=pltpu.VMEM)
    dma = pltpu.SemaphoreType.DMA
    return pl.pallas_call(
        functools.partial(pair_kernel, scale=scale),
        in_specs=[vm] * 8,
        out_specs=[vm] * 5,
        out_shape=[
            jax.ShapeDtypeStruct((size, size), F32), jax.ShapeDtypeStruct(rel_left.shape, BF),
            jax.ShapeDtypeStruct(rel_right.shape, BF), jax.ShapeDtypeStruct(cot_out.shape, F32),
            jax.ShapeDtypeStruct(cot_out.shape, BF),
        ],
        scratch_shapes=Spread.scratch((part, width)) + [dma((1,))],
        compiler_params=pltpu.CompilerParams(
            collective_id=5, has_side_effects=True, vmem_limit_bytes=50 << 20
        ),
        name="pair_head",
    )(emb, rel_left, rel_right, row_panel, col_panel, mask, cot_out, seg_ids)


def norm_back_chunk(g_out, rows, gain):
    average, inverse = norm_stats(rows)
    z = (rows - average) * inverse
    g_z = g_out * gain
    mean_g = jnp.mean(g_z, axis=-1, keepdims=True)
    mean_gz = jnp.mean(g_z * z, axis=-1, keepdims=True)
    return inverse * (g_z - mean_g - z * mean_gz), jnp.sum(g_out * z, axis=0, keepdims=True)


def turn(source, target):
    @pl.loop(0, source.shape[0] // 128, unroll=2)
    def _(c):
        sl = pl.ds(pl.multiple_of(c * 128, 128), 128)
        target[:, sl] = source[sl, :].astype(F32).T.astype(BF)


def put_lines(ref, at, row):
    for j in range(row.shape[1] // 128):
        ref[at + j : at + j + 1, :] = row[:, j * 128 : (j + 1) * 128]


def mlp_back_kernel(*refs, n_ext, units, n_rows, comm, window):
    (slope_ref, wd_ref, wu_ref, gmlp_ref, h2_ref, r1_ref, gy_ref, ctx_ref, wo_ref, gain_ref) = refs[:10]
    at = 10
    arrays = refs[at : at + n_ext]
    at += n_ext
    gup_ref, gr1_ref, gout_ref, gctx_ref, small_ref = refs[at : at + 5]
    at += 5
    carried = refs[at : at + 2]
    at += 2 if comm else 0
    h2_buf, h2t_ref, acc_ref, r1_buf, gy_buf, ctx_buf, ctxt_ref, wo_buf, gatt_ref, in_sem = refs[at : at + 10]
    at += 10
    n_step = pl.num_programs(0)
    step = pl.program_id(0)
    count, feats = acc_ref.shape
    lines = feats // 128
    steps = (small_ref.shape[0] - 16) // lines - 4
    if comm:
        place = Place(n_rows)
        shares = Shares(
            place, units, PIECE, arrays, None, carried, (), (), refs[at : at + 7],
            refs[at + 7 : at + 10], (None, None),
        )
        done = on_the_way(units, 3)

    def inputs():
        pairs = (
            (h2_ref, h2_buf), (ctx_ref, ctx_buf), (r1_ref, r1_buf), (gy_ref, gy_buf), (wo_ref, wo_buf),
        )
        return [pltpu.make_async_copy(a, b, in_sem.at[i]) for i, (a, b) in enumerate(pairs)]

    @pl.when(step == 0)
    def _():
        for copy in inputs():
            copy.start()
        if comm:
            meet(place.peers())
            shares.begin(window)
        acc_ref[...] = jnp.zeros_like(acc_ref)
        small_ref[...] = jnp.zeros_like(small_ref)

    def beat(part):
        if comm:
            by_step(step, 0, steps, lambda n: shares.tick(2 * n + part, window, done))

    g_act = dot(gmlp_ref[...], wd_ref[...], NT)
    g_wide = g_act * slope_ref[...].astype(F32)
    g_u = g_wide.astype(BF)
    bias = jnp.sum(g_u.astype(F32), axis=0, keepdims=True)
    acc_ref[...] += dot(g_u, wu_ref[...], NT)
    beat(0)

    @pl.when(step == 0)
    def _():
        inputs()[0].wait()
        turn(h2_buf, h2t_ref)

    gup_ref[...] = dot(h2t_ref[...], g_u).astype(BF)
    for at_step in range(steps):
        @pl.when(step == at_step)
        def _(at_step=at_step):
            put_lines(small_ref, (4 + at_step) * lines, bias)
    beat(1)

    @pl.when(step == n_step - 1)
    def _():
        for copy in inputs()[1:]:
            copy.wait()
        chunk = 256

        def back(c, sums):
            sl = pl.ds(pl.multiple_of(c * chunk, chunk), chunk)
            g_out = acc_ref[sl, :]
            g_in, part = norm_back_chunk(g_out, r1_buf[sl, :], gain_ref[...].reshape(1, -1))
            g_r1 = gy_buf[sl, :] + g_in
            gr1_ref[sl, :] = g_r1
            gatt_ref[sl, :] = g_r1.astype(BF)
            return sums[0] + part, sums[1] + jnp.sum(g_out, axis=0, keepdims=True)

        nothing = jnp.zeros((1, feats), F32)
        gain_sum, bias_sum = lax.fori_loop(0, count // chunk, back, (nothing, nothing), unroll=2)
        put_lines(small_ref, 2 * lines, gain_sum)
        put_lines(small_ref, 3 * lines, bias_sum)
        if comm:
            shares.tick(2 * steps, window, done)
        turn(ctx_buf, ctxt_ref)
        gctx_ref[...] = dot(gatt_ref[...], wo_buf[...], NT).astype(BF)
        if comm:
            shares.tick(2 * steps + 1, window, done)
        gout_ref[...] = dot(ctxt_ref[...], gatt_ref[...]).astype(BF)
        if comm:
            for t in range(2 * steps + 2, shares.ticks()):
                shares.tick(t, window, done)
            shares.wait_sends()


def early_units():
    order = ((0, 0), (1, 0), (2, 0), (2, 1), (2, 2), (2, 3))
    return tuple(
        Unit(k, s, 0, n % 2 == 0, {0: 1 + n // 2 * 2, 1: 4 + n // 2 * 2}, leave=(n % 2, n // 2))
        for n, (k, s) in enumerate(order)
    )


def mlp_backward(
    slope, w_down, w_up, g_mlp, h2, r1, g_y, ctx, w_out, gain, small_rows, left, right, down, n_rows, comm
):
    count, feats = g_mlp.shape
    hidden = slope.shape[1]
    steps = hidden // feats
    vm = pl.BlockSpec(memory_space=pltpu.VMEM)
    any_ref = pl.BlockSpec(memory_space=pl.ANY)
    views = [view(g, n_rows) for g in (left, right, down)] if comm else []
    units = early_units()
    extra = []
    if comm:
        extra = [
            jax.ShapeDtypeStruct((3, 4, 2, 48, PIECE), BF),
            jax.ShapeDtypeStruct((3, n_rows, 4, 48, PIECE), BF),
        ]
    scratch = [
        pltpu.VMEM((count, feats), BF), pltpu.VMEM((feats, count), BF), pltpu.VMEM((count, feats), F32),
        pltpu.VMEM((count, feats), F32), pltpu.VMEM((count, feats), F32), pltpu.VMEM((count, feats), BF),
        pltpu.VMEM((feats, count), BF), pltpu.VMEM((feats, feats), BF), pltpu.VMEM((count, feats), BF),
        pltpu.SemaphoreType.DMA((5,)),
    ]
    params = dict(vmem_limit_bytes=63 << 20, dimension_semantics=("arbitrary",))
    if comm:
        scratch += Shares.scratch(units, PIECE, n_rows)
        params.update(collective_id=3, has_side_effects=True)
    return pl.pallas_call(
        functools.partial(
            mlp_back_kernel, n_ext=len(views), units=units, n_rows=n_rows, comm=comm, window=2,
        ),
        grid=(steps,),
        in_specs=[
            pl.BlockSpec((count, feats), lambda f: (0, f)),
            pl.BlockSpec((feats, feats), lambda f: (f, 0)),
            pl.BlockSpec((feats, feats), lambda f: (0, f)),
            vm, any_ref, any_ref, any_ref, any_ref, any_ref, vm,
        ] + [any_ref] * len(views),
        out_specs=[pl.BlockSpec((feats, feats), lambda f: (0, f)), vm, vm, vm, vm] + [vm] * len(extra),
        out_shape=[
            jax.ShapeDtypeStruct((feats, hidden), BF), jax.ShapeDtypeStruct((count, feats), F32),
            jax.ShapeDtypeStruct((feats, feats), BF), jax.ShapeDtypeStruct((count, feats), BF),
            jax.ShapeDtypeStruct((small_rows, 128), F32),
        ] + extra,
        scratch_shapes=scratch,
        compiler_params=pltpu.CompilerParams(**params),
        name="mlp_backward",
    )(slope, w_down, w_up, g_mlp, h2, r1, g_y, ctx, w_out, gain, *views)


def deliver_kernel(gx_ref, small_ref, *refs, parts, heads):
    n_in = sum(parts)
    ins, outs = refs[:n_in], refs[n_in:]
    outs[0][...] = gx_ref[...]

    @pl.when(pl.program_id(0) == 0)
    def _():
        at = 0
        for k, n in enumerate(parts):
            out = outs[1 + k]
            row = 0
            for ref in ins[at : at + n]:
                rows, x = ref.shape
                per = x // 128
                for j in range(per):
                    out[pl.ds(row + j, rows, stride=per), :] = ref[:, j * 128 : (j + 1) * 128]
                row += rows * per
            at += n
        line = 0
        for out in outs[1 + len(parts) :]:
            if len(out.shape) == 1:
                for j in range(out.shape[0] // 128):
                    out[j * 128 : (j + 1) * 128] = small_ref[line]
                    line += 1
            else:
                out[...] = small_ref[line : line + out.shape[0], :]


def deliver(g_tokens, small, shares, features, hidden, heads):
    count = g_tokens.shape[0]
    flat = [p for group in shares for p in group]
    vm = pl.BlockSpec(memory_space=pltpu.VMEM)
    block = count // 4
    sizes = [sum(p.size for p in group) for group in shares]
    results = pl.pallas_call(
        functools.partial(deliver_kernel, parts=tuple(len(group) for group in shares), heads=heads),
        grid=(4,),
        in_specs=[pl.BlockSpec((block, features), lambda i: (i, 0)), vm] + [vm] * len(flat),
        out_specs=[pl.BlockSpec((block, features), lambda i: (i, 0))] + [vm] * (len(shares) + 6),
        out_shape=[jax.ShapeDtypeStruct(g_tokens.shape, F32)]
        + [jax.ShapeDtypeStruct((size // 128, 128), F32) for size in sizes]
        + [jax.ShapeDtypeStruct((features,), F32)] * 4
        + [jax.ShapeDtypeStruct((hidden,), F32), jax.ShapeDtypeStruct((heads, 128), F32)],
        name="deliver",
    )(g_tokens, small, *flat)
    return (
        results[0], [r.reshape(-1) for r in results[1 : 1 + len(shares)]], results[1 + len(shares) :]
    )


def back_kernel(*refs, n_ext, units, tail, spans, n_rows, comm, window):
    (q_ref, k_ref, v_ref, e_ref, linv_ref, ctx_ref, gctx_ref, boxr_ref, boxc_ref, w_ref, h1_ref,
     x_ref, gr1_ref, gain_ref, small_ref) = refs[:15]
    at = 15
    arrays = refs[at : at + n_ext]
    at += n_ext
    carried = refs[at : at + 2] if comm else ()
    at += len(carried)
    n_out = len(spans)
    gx_ref = refs[at]
    small_out = refs[at + 1]
    at += 2
    if comm:
        outs = refs[at : at + n_out]
        at += n_out
    else:
        grad_ref = refs[at]
        at += 1
    (oha_ref, ohbt_ref, cx_ref, cy_ref, g_ref, gcx_ref, gcy_ref, lt_ref, gt_ref, gall_ref, h1t_ref,
     hist_ref, h1_buf, x_buf, gr1_buf, w_buf, pack_ref, in_sem) = refs[at : at + 18]
    at += 18
    length = q_ref.shape[0]
    half, quarter = 64, 32
    pairs, seqs = pl.num_programs(0), pl.num_programs(1)
    hp = pl.program_id(0)
    s_id = pl.program_id(1)
    n_seq = cx_ref.shape[0]
    n_pair = hist_ref.shape[0] // 2
    lane = lax.broadcasted_iota(jnp.int32, (1, 128), 1)
    low = lane < 64
    if comm:
        place = Place(n_rows)
        staging = refs[at]
        fins = refs[at + 1 : at + n_out + 1]
        at += n_out + 1
        got = refs[at : at + n_out]
        at += n_out
        known = (None,) * 3 + tuple(arrays) + (None,)
        ends = refs[at : at + 2]
        at += 2
        shares = Shares(
            place, units, PIECE, known, staging, carried, fins, got, refs[at : at + 7],
            refs[at + 7 : at + 10], ends,
        )
        at += 10
        thirds = Shares(
            place, tail, PIECE // 3, known, staging, carried, fins, got, refs[at : at + 7],
            refs[at + 7 : at + 10], ends,
        )
        at += 10
        done = on_the_way(units + tail, n_out)
        total = Total(place, pack_ref, small_out, refs[at : at + 5], refs[at + 5 : at + 7])

    def inputs():
        return (
            pltpu.make_async_copy(h1_ref, h1_buf, in_sem.at[0]),
            pltpu.make_async_copy(x_ref, x_buf, in_sem.at[1]),
            pltpu.make_async_copy(gr1_ref, gr1_buf, in_sem.at[2]),
            pltpu.make_async_copy(w_ref, w_buf, in_sem.at[3]),
        )

    @pl.when((hp == 0) & (s_id == 0))
    def _():
        for copy in inputs():
            copy.start()
        hist_ref[...] = jnp.zeros_like(hist_ref)
        if comm:
            meet(place.peers())
            shares.begin(window)

    @pl.when(hp == 0)
    def _():
        bc = boxc_ref[...]
        ax, _ = key_side(bc[:, 0:1], bc[:, 2:3], half)
        ay, _ = key_side(bc[:, 1:2], bc[:, 3:4], half)
        _, fbx = query_side(bc[:, 0:1], bc[:, 2:3], half)
        _, fby = query_side(bc[:, 1:2], bc[:, 3:4], half)
        spot = (lane % quarter).astype(F32)
        is_x = (lane % half) < quarter
        oha = jnp.where(jnp.where(is_x, ax, ay) == spot, jnp.where(low, 1.0, 0.0), 0.0)
        oha_ref[s_id] = oha.astype(BF)
        br = boxr_ref[...]
        _, gax = key_side(br[0:1], br[2:3], half)
        _, gay = key_side(br[1:2], br[3:4], half)
        rbx, _ = query_side(br[0:1], br[2:3], half)
        rby, _ = query_side(br[1:2], br[3:4], half)
        row = lax.broadcasted_iota(jnp.int32, (half, length), 0)
        rspot = (row % quarter).astype(F32)
        ohbt_ref[s_id] = jnp.where(jnp.where(row < quarter, rbx, rby) == rspot, 1.0, 0.0).astype(BF)
        cx_ref[s_id] = jnp.where(gax + fbx >= SPAN, 1.0, 0.0).astype(BF)
        cy_ref[s_id] = jnp.where(gay + fby >= SPAN, 1.0, 0.0).astype(BF)

    @pl.when((hp == 0) & (s_id == n_seq - 1))
    def _():
        inputs()[0].wait()
        turn(h1_buf, h1t_ref)

    k = k_ref[...]
    v = v_ref[...]
    lt_ref[...] = q_ref[...].astype(F32).T.astype(BF)
    gc = gctx_ref[...].astype(F32) * linv_ref[...]
    gcb = gc.astype(BF)
    gt_ref[...] = gcb.astype(F32).T.astype(BF)
    prod = gc * ctx_ref[...].astype(F32)
    ohbt = ohbt_ref[s_id]
    kts = []
    vts = []
    rows = 256
    n_step = n_pair * n_seq
    step = hp * n_seq + s_id
    for a in range(2):
        if comm and a == 1:
            by_step(step, 0, n_step, lambda n: shares.tick(2 * n, window, done))
        mine = low if a == 0 else jnp.logical_not(low)
        other = 64 - 64 * a
        d = jnp.sum(jnp.where(mine, prod, 0.0), axis=1, keepdims=True)
        dhi = d.astype(BF).astype(F32)
        extra = jnp.where(lane == other, dhi, jnp.where(lane == other + 1, d - dhi, 0.0))
        lhs = jnp.where(mine, gcb.astype(F32), extra).astype(BF)
        minus = jnp.where((lane == other) | (lane == other + 1), -1.0, 0.0).astype(BF)
        rhs = jnp.where(mine, v, minus)
        for c in range(length // rows):
            sl = slice(c * rows, (c + 1) * rows)
            gp = dot(lhs[sl], rhs, NT)
            g = (gp * e_ref[a, sl, :].astype(F32)).astype(BF)
            g_ref[a, sl, :] = g
            gcx_ref[a, sl, :] = g * cx_ref[s_id, sl, :]
            gcy_ref[a, sl, :] = g * cy_ref[s_id, sl, :]
        left = jnp.concatenate([lt_ref[64 * a : 64 * a + 64, :], ohbt], axis=0)
        r0 = dot(left, g_ref[a])
        rx = dot(ohbt[:quarter], gcx_ref[a])
        ry = dot(ohbt[quarter:], gcy_ref[a])
        vts.append(dot(gt_ref[64 * a : 64 * a + 64, :], e_ref[a]))
        kts.append(r0[:64])
        w = jnp.concatenate([r0[64:], rx, ry], axis=0)
        whi, wlo = hi_lo(w)
        red = dot(jnp.concatenate([whi, wlo], axis=0), oha_ref[s_id])
        hist_ref[2 * hp + a] += red[:128] + red[128:]
    zero = jnp.zeros_like(k)
    gq = dot(g_ref[0], jnp.where(low, k, zero)) + dot(g_ref[1], jnp.where(low, zero, k))
    own_rows = pl.ds(pl.multiple_of(s_id * length, length), length)
    feats = h1_buf.shape[1]
    parts = [pl.ds(pl.multiple_of(p * feats + hp * 128, 128), 128) for p in range(3)]
    gall_ref[own_rows, parts[0]] = (gq * 0.125).astype(BF)
    gall_ref[own_rows, parts[1]] = (jnp.concatenate(kts, axis=0) * 0.125).T.astype(BF)
    gall_ref[own_rows, parts[2]] = jnp.concatenate(vts, axis=0).T.astype(BF)

    @pl.when(s_id == n_seq - 1)
    def _():
        g_pair = jnp.concatenate([gall_ref[:, part] for part in parts], axis=1)
        piece = dot(h1t_ref[...], g_pair).astype(BF)
        if comm:
            staging[lax.div(hp, 2), lax.rem(hp, 2)] = piece.reshape(staging.shape[2:])
        else:
            grad_ref[0] = piece[:, :128]
            grad_ref[1] = piece[:, 128:256]
            grad_ref[2] = piece[:, 256:]

    if comm:
        def beat_of(at_step):
            for part in (shares, thirds):
                for i, unit in enumerate(part.units):
                    source = unit.source or ("", 0)
                    if source[0] == "own" and (2 * source[1] + 2) * n_seq - 1 == at_step:
                        part.start(i, 0)
            if at_step < n_step - 1:
                shares.tick(2 * at_step + 1, window, done)

        by_step(step, 0, n_step, beat_of)

    @pl.when((hp == n_pair - 1) & (s_id == n_seq - 1))
    def _():
        for copy in inputs()[1:]:
            copy.wait()
        gain = gain_ref[...].reshape(1, -1)
        count = x_buf.shape[0]
        chunk = 256
        beat = 2 * n_step - 1
        gain_sum = jnp.zeros((1, feats), F32)
        bias_sum = jnp.zeros((1, feats), F32)
        pack_ref[...] = small_ref[...]
        base = pack_ref.shape[0] - 16
        for h in range(2 * n_pair):
            w = hist_ref[h]
            line = jnp.zeros((1, 128), F32)
            for axis in range(2):
                plain = w[axis * quarter : (axis + 1) * quarter]
                carry = w[half + axis * quarter : half + (axis + 1) * quarter]
                keep = (lane >= axis * quarter) & (lane < (axis + 1) * quarter)
                stay = jnp.where(keep, plain - carry, 0.0)
                move = jnp.where(keep, carry, 0.0)
                shift = axis * (half - quarter)
                stay = pltpu.roll(stay, shift, 1, stride=1, stride_axis=0)
                move = pltpu.roll(move, shift + 1, 1, stride=1, stride_axis=0)
                line = line + jnp.sum(stay + move, axis=0, keepdims=True)
            pack_ref[base + h : base + h + 1, :] = line
        for c in range(count // chunk):
            sl = slice(c * chunk, (c + 1) * chunk)
            g_out = dot(gall_ref[sl, :], w_buf[...], NT)
            g_in, part = norm_back_chunk(g_out, x_buf[sl, :].astype(F32), gain)
            gx_ref[sl, :] = gr1_buf[sl, :] + g_in
            gain_sum = gain_sum + part
            bias_sum = bias_sum + jnp.sum(g_out, axis=0, keepdims=True)
            if comm:
                for t in range(beat, beat + 2):
                    shares.tick(t, window, done)
                    thirds.tick(t, window, done)
                beat += 2
        lines = feats // 128
        put_lines(pack_ref, 0, gain_sum)
        put_lines(pack_ref, lines, bias_sum)
        if comm:
            total.start(0)
            stage = 0
            for t in range(beat, max(shares.ticks(), thirds.ticks())):
                shares.tick(t, window, done)
                thirds.tick(t, window, done)
                if t in SUM_BEATS:
                    total.finish(stage)
                    if stage < 3:
                        total.start(stage + 1)
                    stage += 1
            for stage in range(stage, 4):
                total.finish(stage)
                if stage < 3:
                    total.start(stage + 1)
            for n, out in enumerate(outs):
                shares.deliver(n, out, spans[n])
            thirds.wait_sends()
            total.wait_sends()
            shares.wait_sends()
        else:
            small_out[...] = pack_ref[...]


SUM_BEATS = (34, 39, 43, 46)


def late_units():
    rest = ((0, 4, 8), (0, 4, 9), (3, 7, 11), (3, 7, 12), (5, 8, 14), (5, 8, 16))
    units = [
        Unit(
            unit.array, unit.part, 0, unit.rows_first, {"in": enter, 2: second, 3: third},
            source=("mid",) + unit.leave,
        )
        for unit, (enter, second, third) in zip(early_units(), rest)
    ]
    whole = (
        (4, 0, True, (7, 12, 18, 22)), (4, 1, False, (7, 12, 17, 20)), (3, 0, True, (11, 16, 19, 23)),
        (4, 2, False, (11, 16, 23, 28)), (4, 3, True, (22, 27, 33, 42)),
    )
    units += [Unit(k, 0, j, first, dict(enumerate(beats))) for k, j, first, beats in whole]
    own = ((True, (12, 21, 23, 31)), (False, (18, 23, 29, 37)))
    units += [
        Unit(5, 0, t, first, dict(enumerate(beats)), source=("own", t, 0))
        for t, (first, beats) in enumerate(own)
    ]
    thirds = ((True, (27, 32, 38, 44)), (True, (27, 35, 40, 45)), (False, (27, 36, 41, 47)))
    tail = tuple(
        Unit(5, 0, 6 + n, first, dict(enumerate(beats)), source=("own", 2, n * PIECE // 3))
        for n, (first, beats) in enumerate(thirds)
    )
    return tuple(units), tail


def attend_and_project_backward(
    qkv, e, linv, ctx, gctx, boxes_r, boxes_c, weight, h1, tokens, g_r1, gain, small, arrays,
    carried, n_rows, comm
):
    count, width = qkv.shape
    feats = width // 3
    heads, seqs, length, _ = e.shape
    pairs = heads // 2
    rows_of = lambda off: pl.BlockSpec((length, 128), lambda h, s: (s, off + h))
    any_ref = pl.BlockSpec(memory_space=pl.ANY)
    vm = pl.BlockSpec(memory_space=pltpu.VMEM)
    views = [view(g, n_rows) for g in arrays] if comm else []
    n_ext = len(views)
    units, tail = late_units() if comm else ((), ())
    out_shape = [jax.ShapeDtypeStruct((count, feats), F32), jax.ShapeDtypeStruct(small.shape, F32)]
    out_specs = [vm, vm]
    spans = []
    scratch = [
        pltpu.VMEM((seqs, length, 128), BF), pltpu.VMEM((seqs, 64, length), BF),
        pltpu.VMEM((seqs, length, length), BF), pltpu.VMEM((seqs, length, length), BF),
        pltpu.VMEM((2, length, length), BF), pltpu.VMEM((2, length, length), BF),
        pltpu.VMEM((2, length, length), BF), pltpu.VMEM((128, length), BF),
        pltpu.VMEM((128, length), BF), pltpu.VMEM((count, width), BF), pltpu.VMEM((feats, count), BF),
        pltpu.VMEM((heads, 128, 128), F32), pltpu.VMEM((count, feats), BF),
        pltpu.VMEM((count, feats), BF), pltpu.VMEM((count, feats), F32), pltpu.VMEM((feats, width), BF),
        pltpu.VMEM(small.shape, F32), pltpu.SemaphoreType.DMA((4,)),
    ]
    params = dict(vmem_limit_bytes=63 << 20, dimension_semantics=("arbitrary", "arbitrary"))
    if comm:
        hidden = views[-1].shape[5]
        sizes = [(24, feats), (24, feats), (24 * hidden // feats, feats), (24, feats), (24, hidden), (24, width)]
        for rows, x in sizes[:-1]:
            spans.append([(j * 2 * PIECE, PIECE, PIECE) for j in range(x // (2 * PIECE))])
        spans.append(
            [(p * feats + t * 256, 128, 128) for t in range(pairs // 2) for p in range(3)]
        )
        out_shape += [jax.ShapeDtypeStruct(size, F32) for size in sizes]
        out_specs += [vm] * len(sizes)
        tbufs, tsems = Total.scratch(small.shape, n_rows)
        scratch += [pltpu.VMEM((pairs // 2, 2, n_rows, 4, 2, 48, PIECE), BF)]
        scratch += Shares.result_scratch(sizes) + Shares.scratch(units, PIECE, n_rows)
        scratch += Shares.scratch(tail, PIECE // 3, n_rows) + tbufs + tsems
        params.update(collective_id=2, has_side_effects=True)
    else:
        out_shape.append(jax.ShapeDtypeStruct((3, feats, feats), BF))
        out_specs.append(pl.BlockSpec((3, feats, 128), lambda h, s: (0, 0, h)))
    results = pl.pallas_call(
        functools.partial(
            back_kernel, n_ext=n_ext, units=units, tail=tail, spans=spans, n_rows=n_rows, comm=comm, window=2,
        ),
        grid=(pairs, seqs),
        in_specs=[
            rows_of(0), rows_of(pairs), rows_of(2 * pairs),
            pl.BlockSpec((2, None, length, length), lambda h, s: (h, s, 0, 0)),
            rows_of(0), rows_of(0), rows_of(0),
            pl.BlockSpec((4, length), lambda h, s: (0, s)),
            pl.BlockSpec((length, 128), lambda h, s: (s, 0)),
            any_ref, any_ref, any_ref, any_ref, vm, vm,
        ] + [any_ref] * (n_ext + len(carried)),
        out_specs=out_specs,
        out_shape=out_shape,
        scratch_shapes=scratch,
        compiler_params=pltpu.CompilerParams(**params),
        name="attend_backward",
    )(
        qkv, qkv, qkv, e, linv, ctx, gctx, boxes_r, boxes_c, weight, h1, tokens, g_r1,
        gain, small, *views, *carried,
    )
    return results


EPSILON = 1e-05


def norm_stats(rows):
    average = jnp.mean(rows, axis=-1, keepdims=True)
    centred = rows - average
    variance = jnp.mean(centred * centred, axis=-1, keepdims=True)
    return average, lax.rsqrt(variance + EPSILON)


def gelu_pair(u):
    bell = jnp.exp2(u * u * (-0.5 * LOG2E))
    below = 0.5 + 0.5 * lax.erf(u * math.sqrt(0.5))
    return u * below, below + u * bell * (1.0 / math.sqrt(2.0 * math.pi))


def body(
    tokens, boxes, page_ids, seg_ids, pair_mask, ln1_gain, ln1_bias, query_key_value_weight,
    attention_output_weight, ln2_gain, ln2_bias, up_projection_weight, up_projection_bias,
    down_projection_weight, box_table, rel_left, rel_right, cot_out, cot_logits,
):
    features = tokens.shape[1]
    h1, qkv, boxes_c = project_forward(
        tokens, ln1_gain, ln1_bias, query_key_value_weight, boxes, page_ids
    )
    pair_scale = 1.0 / math.sqrt(rel_left.shape[1])
    ctx, e, linv, row_panel, col_panel = attend_forward(
        qkv, boxes, boxes_c, page_ids.shape[0], box_table, pair_mask[0], cot_logits[0], pair_scale
    )
    r1, h2, act, slope, layer_out, embedded = mlp_forward(
        ctx, attention_output_weight, tokens, ln2_gain, ln2_bias, up_projection_weight,
        up_projection_bias, down_projection_weight, seg_ids, SLOTS,
    )
    pair_logits, grad_rel_left, grad_rel_right, g_y, g_mlp = pair_head(
        embedded, rel_left, rel_right, row_panel, col_panel, pair_mask[0], cot_out, seg_ids, pair_scale
    )
    grad_down = dot(act, g_mlp, (((0,), (0,)), ((), ()))).astype(BF)
    n_rows = lax.axis_size("rows")
    comm = n_rows * 8 * 48 <= features
    heads = box_table.shape[0]
    hidden = slope.shape[1]
    small_rows = (4 * features + hidden) // 128 + 16
    grad_up, g_r1, grad_out, g_ctx, small, *early = mlp_backward(
        slope, down_projection_weight, up_projection_weight, g_mlp, h2, r1, g_y, ctx,
        attention_output_weight, ln2_gain, small_rows, grad_rel_left, grad_rel_right, grad_down,
        n_rows, comm,
    )
    g_tokens, small, *late = attend_and_project_backward(
        qkv, e, linv, ctx, g_ctx, boxes, boxes_c, query_key_value_weight, h1, tokens, g_r1, ln1_gain,
        small, (grad_out, grad_up), early, n_rows, comm,
    )
    if comm:
        left, right, down, out, up, qkv_part = late
        shares = [[left], [right], [out], [down], [up], [qkv_part]]
    else:
        grad_qkv = jnp.concatenate([late[0][0], late[0][1], late[0][2]], axis=1)
        flats = [
            lax.psum_scatter(g, AXES, scatter_dimension=0, tiled=True).astype(F32).reshape(-1)
            for g in (grad_rel_left, grad_rel_right, grad_out, grad_down, grad_up, grad_qkv)
        ]
        shares = [[flat.reshape(-1, 128)] for flat in flats]
        small = lax.psum(small, AXES)
    grad_tokens, flats, vectors = deliver(g_tokens, small, shares, features, hidden, heads)
    left_share, right_share, out_share, down_share, up_share, qkv_share = flats
    return (
        layer_out, pair_logits[None], grad_tokens, vectors[0], vectors[1], qkv_share, out_share,
        vectors[2], vectors[3], up_share, vectors[4], down_share, vectors[5], left_share, right_share,
    )


def solution(mesh):
    whole = P(AXES, None)
    tile = P("rows", "gr", "gc")
    flat = P(AXES)
    one = P()
    in_specs = (
        whole, P(None, AXES), whole, whole, tile, one, one, one, one, one, one, one, one, one, one,
        one, one, whole, tile,
    )
    out_specs = (
        whole, tile, whole, one, one, flat, flat, one, one, flat, one, flat, one, flat, flat,
    )
    return jax.shard_map(body, mesh=mesh, in_specs=in_specs, out_specs=out_specs, check_vma=False)
```

profile of v0, /device:TPU:0, one launch (start us, length us, event | category | flops | bytes accessed | tf_op | source)
XLA Modules:
  0.0 238.6 jit_solution(16003239300670727538)
XLA Ops:
  0.6 10.8 %project_forward.1 = (bf16[1024,768]{1,0:T(8,128)(2,1)}, bf16[1024,2304]{1,0:T(8,128)(2,1)}, f32[1024,128]{1,0:T(8,128)}) custom-call(bf16[1024,768]{1,0:T(8,128)(2,1)} %refs_11_.1, f32[768]{0:T(1024)} %refs_13_.1, f32[768]{0:T(1024)} %bias_ref.2, bf16[768,2304]{1,0:T(8,128)(2,1)} %refs_9_.3, s32[4,1024]{1,0:T(4,128)} %refs_7_.1, s32[2,512]{1,0:T(2,128)} %page_ref.1), custom_call_target="tpu_custom_call" | custom-call | tf_op jit(solution)/shard_map/project_forward/pallas_call | solution.py:614
  11.5 0.0 copy-start.8
  11.5 0.0 copy-start.9
  11.5 0.0 copy-start.10
  11.5 39.0 %attend_forward.1 = (bf16[1024,768]{1,0:T(8,128)(2,1)}, bf16[12,2,512,512]{3,2,1,0:T(8,128)(2,1)}, f32[1024,768]{1,0:T(8,128)}, bf16[4,128,512]{2,1,0:T(8,128)(2,1)}, bf16[4,128,512]{2,1,0:T(8,128)(2,1)}) custom-call(bf16[1024,2304]{1,0:T(8,128)(2,1)} %get-tuple-element.62.q_ref.k_ref.v_ref.refs_0_.refs_1_.refs_2_, ...), custom_call_target="tpu_custom_call" | custom-call | tf_op jit(solution)/shard_map/attend_forward/pallas_call | solution.py:170
  50.5 0.0 copy-done
  50.5 0.0 copy-done.7
  50.5 0.0 copy-done.8
  50.6 0.0 copy-start.1
  50.6 0.0 copy-start.5
  50.6 0.0 copy-start.6
  50.6 22.3 %mlp_forward.1 = (f32[1024,768]{1,0:T(8,128)}, bf16[1024,768]{1,0:T(8,128)(2,1)S(1)}, bf16[1024,3072]{1,0:T(8,128)(2,1)}, bf16[1024,3072]{1,0:T(8,128)(2,1)}, bf...) custom-call(bf16[1024,768]{1,0:T(8,128)(2,1)} %get-tuple-element.64.ctx_ref.refs_7_.refs_5_, ...), custom_call_target="tpu_custom_call" | custom-call | tf_op jit(solution)/shard_map/mlp_forward/pallas_call | solution.py:679
  72.9 1.2 copy-done.2
  74.1 0.0 copy-done.1
  74.1 0.0 copy-done.6
  74.1 31.1 %pair_head.1 = (f32[512,512]{1,0:T(8,128)S(1)}, bf16[768,768]{1,0:T(8,128)(2,1)}, bf16[768,768]{1,0:T(8,128)(2,1)}, f32[1024,768]{1,0:T(8,128)}, bf16[1024,768]{1,0:T(8,128)(2,1)}) custom-call(bf16[128,768]{1,0:T(8,128)(2,1)S(1)} %get-tuple-element.66.emb_ref, bf16[768,768]{1,0:T(8,128)(2,1)} %left_ref.1, bf16[768,768]{1,0:T(8,128)(2,1)} %right_ref.1, ...), custom_call_target="tpu_custom_call" | custom-call | tf_op jit(solution)/shard_map/pair_head/pallas_call | solution.py:883
  105.2 0.0 copy-start.3
  105.2 9.5 %convolution_convert_fusion = bf16[3072,768]{1,0:T(8,128)(2,1)} fusion(bf16[1024,3072]{1,0:T(8,128)(2,1)} %get-tuple-element.79, bf16[1024,768]{1,0:T(8,128)(2,1)} %get-tuple-element.73.refs_3_), kind=kOutput, calls=%fused_computation | convolution fusion | flops 4834197504 | bytes 12582912 | tf_op jit(solution)/shard_map/dot_general | solution.py:21
  114.7 0.0 copy-done.3
  114.7 40.6 %mlp_backward.1 = (bf16[768,3072]{1,0:T(8,128)(2,1)}, f32[1024,768]{1,0:T(8,128)}, bf16[768,768]{1,0:T(8,128)(2,1)}, bf16[1024,768]{1,0:T(8,128)(2,1)}, f32[64,1...) custom-call(bf16[1024,3072]{1,0:T(8,128)(2,1)} %get-tuple-element.72.refs_0_, ...), custom_call_target="tpu_custom_call" | custom-call | tf_op jit(solution)/shard_map/mlp_backward/pallas_call | solution.py:1050
  155.3 77.2 %attend_backward.1 = (f32[1024,768]{1,0:T(8,128)}, f32[64,128]{1,0:T(8,128)}, f32[24,768]{1,0:T(8,128)}, f32[24,768]{1,0:T(8,128)}, f32[96,768]{1,0:T(8,128)}, /...) custom-call(bf16[1024,2304]{1,0:T(8,128)(2,1)} %get-tuple-element.62.q_ref.k_ref.v_ref.refs_0_.refs_1_.refs_2_, ...), custom_call_target="tpu_custom_call" | custom-call | tf_op jit(solution)/shard_map/attend_backward/pallas_call | solution.py:1434
  232.5 0.0 copy-start.4
  232.5 5.1 %deliver.1 = (f32[1024,768]{1,0:T(8,128)}, f32[144,128]{1,0:T(8,128)}, f32[144,128]{1,0:T(8,128)}, f32[144,128]{1,0:T(8,128)}, f32[576,128]{1,0:T(8,128)}, /*ind...) custom-call(f32[1024,768]{1,0:T(8,128)} %get-tuple-element.88.gx_ref, ...), custom_call_target="tpu_custom_call" | custom-call | tf_op jit(solution)/shard_map/deliver/pallas_call | solution.py:1107
  237.6 1.0 copy.35
  (7 shorter events, 0.0 us)
Async XLA Ops:
  11.5 39.1 %copy-start = (bf16[768,768]{1,0:T(8,128)(2,1)S(1)}, bf16[768,768]{1,0:T(8,128)(2,1)}, u32[]{:S(2)}) copy-start(bf16[768,768]{1,0:T(8,128)(2,1)} %refs_8_.1) | copy-start | bytes 3538948
  11.5 39.1 %copy-start.7 = (f32[768]{0:T(1024)S(1)}, f32[768]{0:T(1024)}, u32[]{:S(2)}) copy-start(f32[768]{0:T(1024)} %refs_9_.2) | copy-start | bytes 9220
  11.5 39.1 %copy-start.8 = (s32[2,512]{1,0:T(2,128)S(1)}, s32[2,512]{1,0:T(2,128)}, u32[]{:S(2)}) copy-start(s32[2,512]{1,0:T(2,128)} %seg_ref.3) | copy-start | bytes 12292
  11.5 39.1 %copy-start.9 = (f32[3072]{0:T(1024)S(1)}, f32[3072]{0:T(1024)}, u32[]{:S(2)}) copy-start(f32[3072]{0:T(1024)} %param.31) | copy-start | bytes 36868
  11.5 39.1 %copy-start.10 = (f32[768]{0:T(1024)S(1)}, f32[768]{0:T(1024)}, u32[]{:S(2)}) copy-start(f32[768]{0:T(1024)} %bias_ref.3) | copy-start | bytes 9220
  50.6 23.5 %copy-start.1 = (s32[1,512,512]{2,1,0:T(8,128)S(1)}, s32[1,512,512]{2,1,0:T(8,128)}, u32[]{:S(2)}) copy-start(s32[1,512,512]{2,1,0:T(8,128)} %param.23) | copy-start | bytes 3145732
  50.6 23.5 %copy-start.5 = (bf16[4,128,512]{2,1,0:T(8,128)(2,1)S(1)}, bf16[4,128,512]{2,1,0:T(8,128)(2,1)}, u32[]{:S(2)}) copy-start(bf16[4,128,512]{2,1,0:T(8,128)(2,1)} %get-tuple-element.67.rowp_ref) | copy-start | bytes 1572868
  50.6 23.5 %copy-start.6 = (bf16[4,128,512]{2,1,0:T(8,128)(2,1)S(1)}, bf16[4,128,512]{2,1,0:T(8,128)(2,1)}, u32[]{:S(2)}) copy-start(bf16[4,128,512]{2,1,0:T(8,128)(2,1)} %get-tuple-element.68.colp_ref) | copy-start | bytes 1572868
  72.9 1.2 copy-start.2
  105.2 9.5 %copy-start.3 = (f32[512,512]{1,0:T(8,128)}, f32[512,512]{1,0:T(8,128)S(1)}, u32[]{:S(2)}) copy-start(f32[512,512]{1,0:T(8,128)S(1)} %get-tuple-element.69) | copy-start | bytes 3145732
  232.5 5.1 %copy-start.4 = (f32[512,512]{1,0:T(8,128)S(1)}, f32[512,512]{1,0:T(8,128)}, u32[]{:S(2)}) copy-start(f32[512,512]{1,0:T(8,128)} %copy-done.3) | copy-start | bytes 3145732
where the time goes:
time: 239 us
  Pallas kernels  226 us (95%)
  matrix products  9.48 us (4%)
    pallas_call x1, Pallas kernels, attend_and_project_backward(): pl.pallas_call(functools.partial(back_kernel, n_ext=n_ext, units=units, t...  77.2 us
    pallas_call x1, Pallas kernels, mlp_backward(): pl.pallas_call(functools.partial(mlp_back_kernel, n_ext=len(views), units...  40.6 us
    pallas_call x1, Pallas kernels, attend_forward(): pl.pallas_call(functools.partial(fwd_kernel, rows=rows, pair_scale=pair_s...  39 us
    pallas_call x1, Pallas kernels, pair_head(): pl.pallas_call(functools.partial(pair_kernel, scale=scale), in_specs=[vm]...  31.1 us
    pallas_call x1, Pallas kernels, mlp_forward(): pl.pallas_call(mlp_forward_kernel, grid=(hidden // feats,), in_specs=[vm,...  22.3 us
    pallas_call x1, Pallas kernels, project_forward(): pl.pallas_call(project_kernel, grid=(width // block,), in_specs=[pl.Block...  10.8 us
    dot_general x1, matrix products, dot(): return lax.dot_general(a, b, dims, preferred_element_type=F32)  9.48 us
    pallas_call x1, Pallas kernels, deliver(): pl.pallas_call(functools.partial(deliver_kernel, parts=tuple((len(group)...  5.08 us

commit v1 on v0

--- a/solution.py
+++ b/solution.py
@@ -146,8 +146,8 @@
             else:
                 lhs=jnp.concatenate([jnp.where(low,g0,q),jnp.where(low,pg,g0)],axis=1)
             s=dot(lhs,rhs,NT)
-            dxy=dot(lc[:,128:],rxy_ref[...],NT)
-            s=s+cx_ref[sl,:]*dxy[:,:length]+cy_ref[sl,:]*dxy[:,length:]
+            s=s+cx_ref[sl,:]*dot(lc[:,128:],rxy_ref[pl.ds(0,length),:],NT)
+            s=s+cy_ref[sl,:]*dot(lc[:,128:],rxy_ref[pl.ds(length,length),:],NT)
             m=jnp.max(s,axis=1,keepdims=True)
             e=jnp.exp2((s-m)*LOG2E).astype(BF)
             e_ref[a,sl,:]=e
@@ -609,7 +609,7 @@
 def project_forward(tokens, gain, bias, weight, boxes, page_ids):
     count, feats = tokens.shape
     width = weight.shape[1]
-    block = 384
+    block = feats
     vm = pl.BlockSpec(memory_space=pltpu.VMEM)
     return pl.pallas_call(
         project_kernel,
@@ -639,7 +639,7 @@
 ):
     step = pl.program_id(0)
     count = x_ref.shape[0]
-    chunk = 256
+    chunk = 512
 
     @pl.when(step == 0)
     def _():
@@ -927,8 +927,8 @@
     at += 5
     carried = refs[at : at + 2]
     at += 2 if comm else 0
-    h2_buf, h2t_ref, acc_ref, r1_buf, gy_buf, ctx_buf, ctxt_ref, wo_buf, gatt_ref, in_sem = refs[at : at + 10]
-    at += 10
+    h2t_ref, acc_ref, r1_buf, gy_buf, ctx_buf, ctxt_ref, wo_buf, gatt_ref, in_sem = refs[at : at + 9]
+    at += 9
     n_step = pl.num_programs(0)
     step = pl.program_id(0)
     count, feats = acc_ref.shape
@@ -944,7 +944,7 @@
 
     def inputs():
         pairs = (
-            (h2_ref, h2_buf), (ctx_ref, ctx_buf), (r1_ref, r1_buf), (gy_ref, gy_buf), (wo_ref, wo_buf),
+            (ctx_ref, ctx_buf), (r1_ref, r1_buf), (gy_ref, gy_buf), (wo_ref, wo_buf),
         )
         return [pltpu.make_async_copy(a, b, in_sem.at[i]) for i, (a, b) in enumerate(pairs)]
 
@@ -971,8 +971,7 @@
 
     @pl.when(step == 0)
     def _():
-        inputs()[0].wait()
-        turn(h2_buf, h2t_ref)
+        turn(h2_ref, h2t_ref)
 
     gup_ref[...] = dot(h2t_ref[...], g_u).astype(BF)
     for at_step in range(steps):
@@ -983,7 +982,7 @@
 
     @pl.when(step == n_step - 1)
     def _():
-        for copy in inputs()[1:]:
+        for copy in inputs():
             copy.wait()
         chunk = 256
 
@@ -1014,11 +1013,15 @@
 
 
 def early_units():
-    order = ((0, 0), (1, 0), (2, 0), (2, 1), (2, 2), (2, 3))
-    return tuple(
-        Unit(k, s, 0, n % 2 == 0, {0: 1 + n // 2 * 2, 1: 4 + n // 2 * 2}, leave=(n % 2, n // 2))
-        for n, (k, s) in enumerate(order)
-    )
+    order = ((0, 0, False), (1, 0, True), (2, 0, True), (2, 1, False), (2, 2, True), (2, 3, False))
+    left = [0, 0]
+    units = []
+    for n, (k, s, first) in enumerate(order):
+        beats = {0: 1 + n // 2 * 2, 1: 4 + n // 2 * 2}
+        kind = 0 if first else 1
+        units.append(Unit(k, s, 0, first, beats, leave=(kind, left[kind])))
+        left[kind] += 1
+    return tuple(units)
 
 
 def mlp_backward(
@@ -1038,10 +1041,10 @@
             jax.ShapeDtypeStruct((3, n_rows, 4, 48, PIECE), BF),
         ]
     scratch = [
-        pltpu.VMEM((count, feats), BF), pltpu.VMEM((feats, count), BF), pltpu.VMEM((count, feats), F32),
+        pltpu.VMEM((feats, count), BF), pltpu.VMEM((count, feats), F32),
         pltpu.VMEM((count, feats), F32), pltpu.VMEM((count, feats), F32), pltpu.VMEM((count, feats), BF),
         pltpu.VMEM((feats, count), BF), pltpu.VMEM((feats, feats), BF), pltpu.VMEM((count, feats), BF),
-        pltpu.SemaphoreType.DMA((5,)),
+        pltpu.SemaphoreType.DMA((4,)),
     ]
     params = dict(vmem_limit_bytes=63 << 20, dimension_semantics=("arbitrary",))
     if comm:
@@ -1056,7 +1059,7 @@
             pl.BlockSpec((count, feats), lambda f: (0, f)),
             pl.BlockSpec((feats, feats), lambda f: (f, 0)),
             pl.BlockSpec((feats, feats), lambda f: (0, f)),
-            vm, any_ref, any_ref, any_ref, any_ref, any_ref, vm,
+            vm, vm, any_ref, any_ref, any_ref, any_ref, vm,
         ] + [any_ref] * len(views),
         out_specs=[pl.BlockSpec((feats, feats), lambda f: (0, f)), vm, vm, vm, vm] + [vm] * len(extra),
         out_shape=[
@@ -1102,11 +1105,11 @@
     count = g_tokens.shape[0]
     flat = [p for group in shares for p in group]
     vm = pl.BlockSpec(memory_space=pltpu.VMEM)
-    block = count // 4
+    block = count // 2
     sizes = [sum(p.size for p in group) for group in shares]
     results = pl.pallas_call(
         functools.partial(deliver_kernel, parts=tuple(len(group) for group in shares), heads=heads),
-        grid=(4,),
+        grid=(2,),
         in_specs=[pl.BlockSpec((block, features), lambda i: (i, 0)), vm] + [vm] * len(flat),
         out_specs=[pl.BlockSpec((block, features), lambda i: (i, 0))] + [vm] * (len(shares) + 6),
         out_shape=[jax.ShapeDtypeStruct(g_tokens.shape, F32)]
@@ -1355,11 +1358,11 @@
             small_out[...] = pack_ref[...]
 
 
-SUM_BEATS = (34, 39, 43, 46)
+SUM_BEATS = (35, 39, 43, 47)
 
 
 def late_units():
-    rest = ((0, 4, 8), (0, 4, 9), (3, 7, 11), (3, 7, 12), (5, 8, 14), (5, 8, 16))
+    rest = ((0, 4, 7), (3, 8, 17), (0, 4, 9), (3, 8, 15), (1, 6, 13), (1, 6, 11))
     units = [
         Unit(
             unit.array, unit.part, 0, unit.rows_first, {"in": enter, 2: second, 3: third},
@@ -1368,16 +1371,16 @@
         for unit, (enter, second, third) in zip(early_units(), rest)
     ]
     whole = (
-        (4, 0, True, (7, 12, 18, 22)), (4, 1, False, (7, 12, 17, 20)), (3, 0, True, (11, 16, 19, 23)),
-        (4, 2, False, (11, 16, 23, 28)), (4, 3, True, (22, 27, 33, 42)),
+        (4, 0, True, (5, 12, 18, 21)), (4, 1, True, (9, 16, 20, 23)), (3, 0, False, (5, 12, 22, 23)),
+        (4, 2, False, (9, 16, 23, 29)), (4, 3, True, (21, 27, 34, 44)),
     )
     units += [Unit(k, 0, j, first, dict(enumerate(beats))) for k, j, first, beats in whole]
-    own = ((True, (12, 21, 23, 31)), (False, (18, 23, 29, 37)))
+    own = ((True, (10, 20, 25, 32)), (False, (19, 23, 31, 38)))
     units += [
         Unit(5, 0, t, first, dict(enumerate(beats)), source=("own", t, 0))
         for t, (first, beats) in enumerate(own)
     ]
-    thirds = ((True, (27, 32, 38, 44)), (True, (27, 35, 40, 45)), (False, (27, 36, 41, 47)))
+    thirds = ((True, (27, 33, 40, 45)), (False, (27, 37, 42, 48)), (True, (27, 36, 41, 46)))
     tail = tuple(
         Unit(5, 0, 6 + n, first, dict(enumerate(beats)), source=("own", 2, n * PIECE // 3))
         for n, (first, beats) in enumerate(thirds)
@@ -1433,7 +1436,7 @@
         out_specs.append(pl.BlockSpec((3, feats, 128), lambda h, s: (0, 0, h)))
     results = pl.pallas_call(
         functools.partial(
-            back_kernel, n_ext=n_ext, units=units, tail=tail, spans=spans, n_rows=n_rows, comm=comm, window=2,
+            back_kernel, n_ext=n_ext, units=units, tail=tail, spans=spans, n_rows=n_rows, comm=comm, window=3,
         ),
         grid=(pairs, seqs),
         in_specs=[

time: 239 us -> 236 us (0.987)
  Pallas kernels: 226 us -> 223 us
where the time goes in v1:
time: 236 us
  Pallas kernels  223 us (94%)
  matrix products  9.48 us (4%)
    pallas_call x1, Pallas kernels, attend_and_project_backward(): pl.pallas_call(functools.partial(back_kernel, n_ext=n_ext, units=units, t...  78.1 us
    pallas_call x1, Pallas kernels, mlp_backward(): pl.pallas_call(functools.partial(mlp_back_kernel, n_ext=len(views), units...  41.1 us
    pallas_call x1, Pallas kernels, attend_forward(): pl.pallas_call(functools.partial(fwd_kernel, rows=rows, pair_scale=pair_s...  37.8 us
    pallas_call x1, Pallas kernels, pair_head(): pl.pallas_call(functools.partial(pair_kernel, scale=scale), in_specs=[vm]...  31.1 us
    pallas_call x1, Pallas kernels, mlp_forward(): pl.pallas_call(mlp_forward_kernel, grid=(hidden // feats,), in_specs=[vm,...  21.9 us
    dot_general x1, matrix products, dot(): return lax.dot_general(a, b, dims, preferred_element_type=F32)  9.48 us
    pallas_call x1, Pallas kernels, project_forward(): pl.pallas_call(project_kernel, grid=(width // block,), in_specs=[pl.Block...  9.15 us

profile of v1, /device:TPU:0, one launch (start us, length us, event | category | flops | bytes accessed | tf_op | source)
XLA Modules:
  0.0 235.7 jit_solution(6962549867650934059)
XLA Ops:
  0.6 9.1 %project_forward.1 = (bf16[1024,768]{1,0:T(8,128)(2,1)}, bf16[1024,2304]{1,0:T(8,128)(2,1)}, f32[1024,128]{1,0:T(8,128)}) custom-call(bf16[1024,768]{1,0:T(8,128)(2,1)} %refs_11_.1, f32[768]{0:T(1024)} %refs_13_.1, f32[768]{0:T(1024)} %bias_ref.2, bf16[768,2304]{1,0:T(8,128)(2,1)} %refs_9_.3, s32[4,1024]{1,0:T(4,128)} %refs_7_.1, s32[2,512]{1,0:T(2,128)} %page_ref.1), custom_call_target="tpu_custom_call" | custom-call | tf_op jit(solution)/shard_map/project_forward/pallas_call | solution.py:614
  9.8 0.0 copy-start.8
  9.8 0.0 copy-start.9
  9.8 0.0 copy-start.10
  9.8 37.8 %attend_forward.1 = (bf16[1024,768]{1,0:T(8,128)(2,1)}, bf16[12,2,512,512]{3,2,1,0:T(8,128)(2,1)}, f32[1024,768]{1,0:T(8,128)}, bf16[4,128,512]{2,1,0:T(8,128)(2,1)}, bf16[4,128,512]{2,1,0:T(8,128)(2,1)}) custom-call(bf16[1024,2304]{1,0:T(8,128)(2,1)} %get-tuple-element.62.q_ref.k_ref.v_ref.refs_0_.refs_1_.refs_2_, ...), custom_call_target="tpu_custom_call" | custom-call | tf_op jit(solution)/shard_map/attend_forward/pallas_call | solution.py:170
  47.7 0.0 copy-done
  47.7 0.0 copy-done.7
  47.7 0.0 copy-done.8
  47.7 0.0 copy-done.9
  47.7 0.0 copy-done.10
  47.7 0.0 copy-start.1
  47.7 0.0 copy-start.5
  47.8 0.0 copy-start.6
  47.8 21.9 %mlp_forward.1 = (f32[1024,768]{1,0:T(8,128)}, bf16[1024,768]{1,0:T(8,128)(2,1)S(1)}, bf16[1024,3072]{1,0:T(8,128)(2,1)}, bf16[1024,3072]{1,0:T(8,128)(2,1)}, bf...) custom-call(bf16[1024,768]{1,0:T(8,128)(2,1)} %get-tuple-element.64.ctx_ref.refs_7_.refs_5_, ...), custom_call_target="tpu_custom_call" | custom-call | tf_op jit(solution)/shard_map/mlp_forward/pallas_call | solution.py:679
  69.7 1.2 copy-done.2
  70.9 31.1 %pair_head.1 = (f32[512,512]{1,0:T(8,128)S(1)}, bf16[768,768]{1,0:T(8,128)(2,1)}, bf16[768,768]{1,0:T(8,128)(2,1)}, f32[1024,768]{1,0:T(8,128)}, bf16[1024,768]{1,0:T(8,128)(2,1)}) custom-call(bf16[128,768]{1,0:T(8,128)(2,1)S(1)} %get-tuple-element.66.emb_ref, bf16[768,768]{1,0:T(8,128)(2,1)} %left_ref.1, bf16[768,768]{1,0:T(8,128)(2,1)} %right_ref.1, ...), custom_call_target="tpu_custom_call" | custom-call | tf_op jit(solution)/shard_map/pair_head/pallas_call | solution.py:883
  102.0 0.0 copy-start.3
  102.0 9.5 %convolution_convert_fusion = bf16[3072,768]{1,0:T(8,128)(2,1)} fusion(bf16[1024,3072]{1,0:T(8,128)(2,1)} %get-tuple-element.79, bf16[1024,768]{1,0:T(8,128)(2,1)} %get-tuple-element.73.refs_3_), kind=kOutput, calls=%fused_computation | convolution fusion | flops 4834197504 | bytes 12582912 | tf_op jit(solution)/shard_map/dot_general | solution.py:21
  111.5 0.0 copy-done.3
  111.5 41.1 %mlp_backward.1 = (bf16[768,3072]{1,0:T(8,128)(2,1)}, f32[1024,768]{1,0:T(8,128)}, bf16[768,768]{1,0:T(8,128)(2,1)}, bf16[1024,768]{1,0:T(8,128)(2,1)}, f32[64,1...) custom-call(bf16[1024,3072]{1,0:T(8,128)(2,1)} %get-tuple-element.72.refs_0_, ...), custom_call_target="tpu_custom_call" | custom-call | tf_op jit(solution)/shard_map/mlp_backward/pallas_call | solution.py:1053
  152.6 78.1 %attend_backward.1 = (f32[1024,768]{1,0:T(8,128)}, f32[64,128]{1,0:T(8,128)}, f32[24,768]{1,0:T(8,128)}, f32[24,768]{1,0:T(8,128)}, f32[96,768]{1,0:T(8,128)}, /...) custom-call(bf16[1024,2304]{1,0:T(8,128)(2,1)} %get-tuple-element.62.q_ref.k_ref.v_ref.refs_0_.refs_1_.refs_2_, ...), custom_call_target="tpu_custom_call" | custom-call | tf_op jit(solution)/shard_map/attend_backward/pallas_call | solution.py:1437
  230.7 0.0 copy-start.4
  230.7 4.0 %deliver.1 = (f32[1024,768]{1,0:T(8,128)}, f32[144,128]{1,0:T(8,128)}, f32[144,128]{1,0:T(8,128)}, f32[144,128]{1,0:T(8,128)}, f32[576,128]{1,0:T(8,128)}, /*ind...) custom-call(f32[1024,768]{1,0:T(8,128)} %get-tuple-element.88.gx_ref, ...), custom_call_target="tpu_custom_call" | custom-call | tf_op jit(solution)/shard_map/deliver/pallas_call | solution.py:1110
  234.8 1.0 copy.35
  (7 shorter events, 0.0 us)
Async XLA Ops:
  9.8 37.9 %copy-start = (bf16[768,768]{1,0:T(8,128)(2,1)S(1)}, bf16[768,768]{1,0:T(8,128)(2,1)}, u32[]{:S(2)}) copy-start(bf16[768,768]{1,0:T(8,128)(2,1)} %refs_8_.1) | copy-start | bytes 3538948
  9.8 37.9 %copy-start.7 = (f32[768]{0:T(1024)S(1)}, f32[768]{0:T(1024)}, u32[]{:S(2)}) copy-start(f32[768]{0:T(1024)} %refs_9_.2) | copy-start | bytes 9220
  9.8 37.9 %copy-start.8 = (s32[2,512]{1,0:T(2,128)S(1)}, s32[2,512]{1,0:T(2,128)}, u32[]{:S(2)}) copy-start(s32[2,512]{1,0:T(2,128)} %seg_ref.3) | copy-start | bytes 12292
  9.8 37.9 %copy-start.9 = (f32[3072]{0:T(1024)S(1)}, f32[3072]{0:T(1024)}, u32[]{:S(2)}) copy-start(f32[3072]{0:T(1024)} %param.31) | copy-start | bytes 36868
  9.8 37.9 %copy-start.10 = (f32[768]{0:T(1024)S(1)}, f32[768]{0:T(1024)}, u32[]{:S(2)}) copy-start(f32[768]{0:T(1024)} %bias_ref.3) | copy-start | bytes 9220
  47.7 23.1 %copy-start.1 = (s32[1,512,512]{2,1,0:T(8,128)S(1)}, s32[1,512,512]{2,1,0:T(8,128)}, u32[]{:S(2)}) copy-start(s32[1,512,512]{2,1,0:T(8,128)} %param.23) | copy-start | bytes 3145732
  47.7 23.1 %copy-start.5 = (bf16[4,128,512]{2,1,0:T(8,128)(2,1)S(1)}, bf16[4,128,512]{2,1,0:T(8,128)(2,1)}, u32[]{:S(2)}) copy-start(bf16[4,128,512]{2,1,0:T(8,128)(2,1)} %get-tuple-element.67.rowp_ref) | copy-start | bytes 1572868
  47.8 23.1 %copy-start.6 = (bf16[4,128,512]{2,1,0:T(8,128)(2,1)S(1)}, bf16[4,128,512]{2,1,0:T(8,128)(2,1)}, u32[]{:S(2)}) copy-start(bf16[4,128,512]{2,1,0:T(8,128)(2,1)} %get-tuple-element.68.colp_ref) | copy-start | bytes 1572868
  69.7 1.2 copy-start.2
  102.0 9.5 %copy-start.3 = (f32[512,512]{1,0:T(8,128)}, f32[512,512]{1,0:T(8,128)S(1)}, u32[]{:S(2)}) copy-start(f32[512,512]{1,0:T(8,128)S(1)} %get-tuple-element.69) | copy-start | bytes 3145732
  230.7 4.1 %copy-start.4 = (f32[512,512]{1,0:T(8,128)S(1)}, f32[512,512]{1,0:T(8,128)}, u32[]{:S(2)}) copy-start(f32[512,512]{1,0:T(8,128)} %copy-done.3) | copy-start | bytes 3145732

commit v2 on v1

--- a/solution.py
+++ b/solution.py
@@ -907,7 +907,7 @@
 
 
 def turn(source, target):
-    @pl.loop(0, source.shape[0] // 128, unroll=2)
+    @pl.loop(0, source.shape[0] // 128)
     def _(c):
         sl = pl.ds(pl.multiple_of(c * 128, 128), 128)
         target[:, sl] = source[sl, :].astype(F32).T.astype(BF)
@@ -925,8 +925,8 @@
     at += n_ext
     gup_ref, gr1_ref, gout_ref, gctx_ref, small_ref = refs[at : at + 5]
     at += 5
-    carried = refs[at : at + 2]
-    at += 2 if comm else 0
+    carried = refs[at : at + 3]
+    at += 3 if comm else 0
     h2t_ref, acc_ref, r1_buf, gy_buf, ctx_buf, ctxt_ref, wo_buf, gatt_ref, in_sem = refs[at : at + 9]
     at += 9
     n_step = pl.num_programs(0)
@@ -996,7 +996,7 @@
             return sums[0] + part, sums[1] + jnp.sum(g_out, axis=0, keepdims=True)
 
         nothing = jnp.zeros((1, feats), F32)
-        gain_sum, bias_sum = lax.fori_loop(0, count // chunk, back, (nothing, nothing), unroll=2)
+        gain_sum, bias_sum = lax.fori_loop(0, count // chunk, back, (nothing, nothing))
         put_lines(small_ref, 2 * lines, gain_sum)
         put_lines(small_ref, 3 * lines, bias_sum)
         if comm:
@@ -1013,15 +1013,14 @@
 
 
 def early_units():
-    order = ((0, 0, False), (1, 0, True), (2, 0, True), (2, 1, False), (2, 2, True), (2, 3, False))
-    left = [0, 0]
-    units = []
-    for n, (k, s, first) in enumerate(order):
-        beats = {0: 1 + n // 2 * 2, 1: 4 + n // 2 * 2}
-        kind = 0 if first else 1
-        units.append(Unit(k, s, 0, first, beats, leave=(kind, left[kind])))
-        left[kind] += 1
-    return tuple(units)
+    return (
+        Unit(0, 0, 0, False, {0: 1, 1: 4, 2: 7}, leave=(2, 0)),
+        Unit(1, 0, 0, True, {0: 1, 1: 4, 2: 7}, leave=(2, 1)),
+        Unit(2, 0, 0, False, {0: 2, 1: 6}, leave=(1, 0)),
+        Unit(2, 1, 0, True, {0: 2, 1: 6}, leave=(0, 0)),
+        Unit(2, 2, 0, False, {0: 5, 1: 9}, leave=(1, 1)),
+        Unit(2, 3, 0, True, {0: 5, 1: 9}, leave=(0, 1)),
+    )
 
 
 def mlp_backward(
@@ -1037,8 +1036,9 @@
     extra = []
     if comm:
         extra = [
-            jax.ShapeDtypeStruct((3, 4, 2, 48, PIECE), BF),
-            jax.ShapeDtypeStruct((3, n_rows, 4, 48, PIECE), BF),
+            jax.ShapeDtypeStruct((2, 4, 2, 48, PIECE), BF),
+            jax.ShapeDtypeStruct((2, n_rows, 4, 48, PIECE), BF),
+            jax.ShapeDtypeStruct((2, 4, 48, PIECE), BF),
         ]
     scratch = [
         pltpu.VMEM((feats, count), BF), pltpu.VMEM((count, feats), F32),
@@ -1052,7 +1052,7 @@
         params.update(collective_id=3, has_side_effects=True)
     return pl.pallas_call(
         functools.partial(
-            mlp_back_kernel, n_ext=len(views), units=units, n_rows=n_rows, comm=comm, window=2,
+            mlp_back_kernel, n_ext=len(views), units=units, n_rows=n_rows, comm=comm, window=3,
         ),
         grid=(steps,),
         in_specs=[
@@ -1129,7 +1129,7 @@
     at = 15
     arrays = refs[at : at + n_ext]
     at += n_ext
-    carried = refs[at : at + 2] if comm else ()
+    carried = refs[at : at + 3] if comm else ()
     at += len(carried)
     n_out = len(spans)
     gx_ref = refs[at]
@@ -1358,32 +1358,37 @@
             small_out[...] = pack_ref[...]
 
 
-SUM_BEATS = (35, 39, 43, 47)
+SUM_BEATS = (34, 38, 43, 47)
 
 
 def late_units():
-    rest = ((0, 4, 7), (3, 8, 17), (0, 4, 9), (3, 8, 15), (1, 6, 13), (1, 6, 11))
+    rest = (
+        {'in': 2, 3: 6},
+        {'in': 0, 3: 4},
+        {'in': 0, 2: 4, 3: 8},
+        {'in': 0, 2: 4, 3: 10},
+        {'in': 2, 2: 6, 3: 12},
+        {'in': 2, 2: 6, 3: 14},
+    )
     units = [
         Unit(
-            unit.array, unit.part, 0, unit.rows_first, {"in": enter, 2: second, 3: third},
-            source=("mid",) + unit.leave,
+            unit.array, unit.part, 0, unit.rows_first, beats, source=("mid",) + unit.leave
         )
-        for unit, (enter, second, third) in zip(early_units(), rest)
+        for unit, beats in zip(early_units(), rest)
     ]
-    whole = (
-        (4, 0, True, (5, 12, 18, 21)), (4, 1, True, (9, 16, 20, 23)), (3, 0, False, (5, 12, 22, 23)),
-        (4, 2, False, (9, 16, 23, 29)), (4, 3, True, (21, 27, 34, 44)),
-    )
-    units += [Unit(k, 0, j, first, dict(enumerate(beats))) for k, j, first, beats in whole]
-    own = ((True, (10, 20, 25, 32)), (False, (19, 23, 31, 38)))
     units += [
-        Unit(5, 0, t, first, dict(enumerate(beats)), source=("own", t, 0))
-        for t, (first, beats) in enumerate(own)
+        Unit(4, 0, 0, True, {0: 4, 1: 10, 2: 16, 3: 20}),
+        Unit(4, 0, 1, False, {0: 4, 1: 10, 2: 16, 3: 22}),
+        Unit(3, 0, 0, True, {0: 8, 1: 14, 2: 22, 3: 25}),
+        Unit(4, 0, 2, False, {0: 8, 1: 14, 2: 18, 3: 23}),
+        Unit(4, 0, 3, True, {0: 16, 1: 22, 2: 25, 3: 31}),
+        Unit(5, 0, 0, False, {0: 11, 1: 20, 2: 27, 3: 36}, source=("own", 0, 0)),
+        Unit(5, 0, 1, True, {0: 19, 1: 25, 2: 32, 3: 41}, source=("own", 1, 0)),
     ]
-    thirds = ((True, (27, 33, 40, 45)), (False, (27, 37, 42, 48)), (True, (27, 36, 41, 46)))
-    tail = tuple(
-        Unit(5, 0, 6 + n, first, dict(enumerate(beats)), source=("own", 2, n * PIECE // 3))
-        for n, (first, beats) in enumerate(thirds)
+    tail = (
+        Unit(5, 0, 6, False, {0: 26, 1: 35, 2: 39, 3: 44}, source=("own", 2, 0 * PIECE // 3)),
+        Unit(5, 0, 7, False, {0: 27, 1: 37, 2: 42, 3: 46}, source=("own", 2, 1 * PIECE // 3)),
+        Unit(5, 0, 8, True, {0: 27, 1: 33, 2: 40, 3: 45}, source=("own", 2, 2 * PIECE // 3)),
     )
     return tuple(units), tail
 

time: 236 us -> 230 us (0.975)
  Pallas kernels: 223 us -> 217 us
    pallas_call x1, Pallas kernels: 78.1 us -> 70.4 us  [attend_and_project_backward(): pl.pallas_call(functools.partial(back_kernel, n_ext=n_ext, units=units, t...]
where the time goes in v2:
time: 230 us
  Pallas kernels  217 us (94%)
  matrix products  9.48 us (4%)
    pallas_call x1, Pallas kernels, attend_and_project_backward(): pl.pallas_call(functools.partial(back_kernel, n_ext=n_ext, units=units, t...  70.4 us
    pallas_call x1, Pallas kernels, mlp_backward(): pl.pallas_call(functools.partial(mlp_back_kernel, n_ext=len(views), units...  42.8 us
    pallas_call x1, Pallas kernels, attend_forward(): pl.pallas_call(functools.partial(fwd_kernel, rows=rows, pair_scale=pair_s...  37.8 us
    pallas_call x1, Pallas kernels, pair_head(): pl.pallas_call(functools.partial(pair_kernel, scale=scale), in_specs=[vm]...  31.1 us
    pallas_call x1, Pallas kernels, mlp_forward(): pl.pallas_call(mlp_forward_kernel, grid=(hidden // feats,), in_specs=[vm,...  21.9 us
    dot_general x1, matrix products, dot(): return lax.dot_general(a, b, dims, preferred_element_type=F32)  9.48 us
    pallas_call x1, Pallas kernels, project_forward(): pl.pallas_call(project_kernel, grid=(width // block,), in_specs=[pl.Block...  9.15 us

profile of v2, /device:TPU:0, one launch (start us, length us, event | category | flops | bytes accessed | tf_op | source)
XLA Modules:
  0.0 229.8 jit_solution(4531733935589187550)
XLA Ops:
  0.6 9.1 %project_forward.1 = (bf16[1024,768]{1,0:T(8,128)(2,1)}, bf16[1024,2304]{1,0:T(8,128)(2,1)}, f32[1024,128]{1,0:T(8,128)}) custom-call(bf16[1024,768]{1,0:T(8,128)(2,1)} %refs_11_.1, f32[768]{0:T(1024)} %refs_13_.1, f32[768]{0:T(1024)} %bias_ref.2, bf16[768,2304]{1,0:T(8,128)(2,1)} %refs_9_.3, s32[4,1024]{1,0:T(4,128)} %refs_7_.1, s32[2,512]{1,0:T(2,128)} %page_ref.1), custom_call_target="tpu_custom_call" | custom-call | tf_op jit(solution)/shard_map/project_forward/pallas_call | solution.py:614
  9.8 0.0 copy-start.8
  9.8 0.0 copy-start.9
  9.8 0.0 copy-start.10
  9.8 37.8 %attend_forward.1 = (bf16[1024,768]{1,0:T(8,128)(2,1)}, bf16[12,2,512,512]{3,2,1,0:T(8,128)(2,1)}, f32[1024,768]{1,0:T(8,128)}, bf16[4,128,512]{2,1,0:T(8,128)(2,1)}, bf16[4,128,512]{2,1,0:T(8,128)(2,1)}) custom-call(bf16[1024,2304]{1,0:T(8,128)(2,1)} %get-tuple-element.63.q_ref.k_ref.v_ref.refs_0_.refs_1_.refs_2_, ...), custom_call_target="tpu_custom_call" | custom-call | tf_op jit(solution)/shard_map/attend_forward/pallas_call | solution.py:170
  47.7 0.0 copy-done
  47.7 0.0 copy-done.7
  47.7 0.0 copy-done.8
  47.7 0.0 copy-done.9
  47.7 0.0 copy-done.10
  47.7 0.0 copy-start.1
  47.7 0.0 copy-start.5
  47.8 0.0 copy-start.6
  47.8 21.9 %mlp_forward.1 = (f32[1024,768]{1,0:T(8,128)}, bf16[1024,768]{1,0:T(8,128)(2,1)S(1)}, bf16[1024,3072]{1,0:T(8,128)(2,1)}, bf16[1024,3072]{1,0:T(8,128)(2,1)}, bf...) custom-call(bf16[1024,768]{1,0:T(8,128)(2,1)} %get-tuple-element.65.ctx_ref.refs_7_.refs_5_, ...), custom_call_target="tpu_custom_call" | custom-call | tf_op jit(solution)/shard_map/mlp_forward/pallas_call | solution.py:679
  69.7 1.2 copy-done.2
  70.9 0.0 copy-done.5
  70.9 31.1 %pair_head.1 = (f32[512,512]{1,0:T(8,128)S(1)}, bf16[768,768]{1,0:T(8,128)(2,1)}, bf16[768,768]{1,0:T(8,128)(2,1)}, f32[1024,768]{1,0:T(8,128)}, bf16[1024,768]{1,0:T(8,128)(2,1)}) custom-call(bf16[128,768]{1,0:T(8,128)(2,1)S(1)} %get-tuple-element.67.emb_ref, bf16[768,768]{1,0:T(8,128)(2,1)} %left_ref.1, bf16[768,768]{1,0:T(8,128)(2,1)} %right_ref.1, ...), custom_call_target="tpu_custom_call" | custom-call | tf_op jit(solution)/shard_map/pair_head/pallas_call | solution.py:883
  102.0 0.0 copy-start.3
  102.0 9.5 %convolution_convert_fusion = bf16[3072,768]{1,0:T(8,128)(2,1)} fusion(bf16[1024,3072]{1,0:T(8,128)(2,1)} %get-tuple-element.80, bf16[1024,768]{1,0:T(8,128)(2,1)} %get-tuple-element.74.refs_3_), kind=kOutput, calls=%fused_computation | convolution fusion | flops 4834197504 | bytes 12582912 | tf_op jit(solution)/shard_map/dot_general | solution.py:21
  111.5 42.8 %mlp_backward.1 = (bf16[768,3072]{1,0:T(8,128)(2,1)}, f32[1024,768]{1,0:T(8,128)}, bf16[768,768]{1,0:T(8,128)(2,1)}, bf16[1024,768]{1,0:T(8,128)(2,1)}, f32[64,1...) custom-call(bf16[1024,3072]{1,0:T(8,128)(2,1)} %get-tuple-element.73, ...), custom_call_target="tpu_custom_call" | custom-call | tf_op jit(solution)/shard_map/mlp_backward/pallas_call | solution.py:1053
  154.3 70.4 %attend_backward.1 = (f32[1024,768]{1,0:T(8,128)}, f32[64,128]{1,0:T(8,128)}, f32[24,768]{1,0:T(8,128)}, f32[24,768]{1,0:T(8,128)}, f32[96,768]{1,0:T(8,128)}, /...) custom-call(bf16[1024,2304]{1,0:T(8,128)(2,1)} %get-tuple-element.63.q_ref.k_ref.v_ref.refs_0_.refs_1_.refs_2_, ...), custom_call_target="tpu_custom_call" | custom-call | tf_op jit(solution)/shard_map/attend_backward/pallas_call | solution.py:1442
  224.7 0.0 copy-start.4
  224.7 4.0 %deliver.1 = (f32[1024,768]{1,0:T(8,128)}, f32[144,128]{1,0:T(8,128)}, f32[144,128]{1,0:T(8,128)}, f32[144,128]{1,0:T(8,128)}, f32[576,128]{1,0:T(8,128)}, /*ind...) custom-call(f32[1024,768]{1,0:T(8,128)} %get-tuple-element.90.gx_ref, ...), custom_call_target="tpu_custom_call" | custom-call | tf_op jit(solution)/shard_map/deliver/pallas_call | solution.py:1110
  228.8 1.0 copy.35
  (7 shorter events, 0.0 us)
Async XLA Ops:
  9.8 37.9 %copy-start = (bf16[768,768]{1,0:T(8,128)(2,1)S(1)}, bf16[768,768]{1,0:T(8,128)(2,1)}, u32[]{:S(2)}) copy-start(bf16[768,768]{1,0:T(8,128)(2,1)} %refs_8_.1) | copy-start | bytes 3538948
  9.8 37.9 %copy-start.7 = (f32[768]{0:T(1024)S(1)}, f32[768]{0:T(1024)}, u32[]{:S(2)}) copy-start(f32[768]{0:T(1024)} %refs_9_.2) | copy-start | bytes 9220
  9.8 37.9 %copy-start.8 = (s32[2,512]{1,0:T(2,128)S(1)}, s32[2,512]{1,0:T(2,128)}, u32[]{:S(2)}) copy-start(s32[2,512]{1,0:T(2,128)} %seg_ref.3) | copy-start | bytes 12292
  9.8 37.9 %copy-start.9 = (f32[3072]{0:T(1024)S(1)}, f32[3072]{0:T(1024)}, u32[]{:S(2)}) copy-start(f32[3072]{0:T(1024)} %param.31) | copy-start | bytes 36868
  9.8 37.9 %copy-start.10 = (f32[768]{0:T(1024)S(1)}, f32[768]{0:T(1024)}, u32[]{:S(2)}) copy-start(f32[768]{0:T(1024)} %bias_ref.3) | copy-start | bytes 9220
  47.7 23.1 %copy-start.1 = (s32[1,512,512]{2,1,0:T(8,128)S(1)}, s32[1,512,512]{2,1,0:T(8,128)}, u32[]{:S(2)}) copy-start(s32[1,512,512]{2,1,0:T(8,128)} %param.23) | copy-start | bytes 3145732
  47.7 23.1 %copy-start.5 = (bf16[4,128,512]{2,1,0:T(8,128)(2,1)S(1)}, bf16[4,128,512]{2,1,0:T(8,128)(2,1)}, u32[]{:S(2)}) copy-start(bf16[4,128,512]{2,1,0:T(8,128)(2,1)} %get-tuple-element.68.rowp_ref) | copy-start | bytes 1572868
  47.8 23.1 %copy-start.6 = (bf16[4,128,512]{2,1,0:T(8,128)(2,1)S(1)}, bf16[4,128,512]{2,1,0:T(8,128)(2,1)}, u32[]{:S(2)}) copy-start(bf16[4,128,512]{2,1,0:T(8,128)(2,1)} %get-tuple-element.69.colp_ref) | copy-start | bytes 1572868
  69.7 1.2 copy-start.2
  102.0 9.5 %copy-start.3 = (f32[512,512]{1,0:T(8,128)}, f32[512,512]{1,0:T(8,128)S(1)}, u32[]{:S(2)}) copy-start(f32[512,512]{1,0:T(8,128)S(1)} %get-tuple-element.70) | copy-start | bytes 3145732
  224.7 4.1 %copy-start.4 = (f32[512,512]{1,0:T(8,128)S(1)}, f32[512,512]{1,0:T(8,128)}, u32[]{:S(2)}) copy-start(f32[512,512]{1,0:T(8,128)} %copy-done.3) | copy-start | bytes 3145732

commit v3 on v2

--- a/solution.py
+++ b/solution.py
@@ -1105,11 +1105,11 @@
     count = g_tokens.shape[0]
     flat = [p for group in shares for p in group]
     vm = pl.BlockSpec(memory_space=pltpu.VMEM)
-    block = count // 2
+    block = count
     sizes = [sum(p.size for p in group) for group in shares]
     results = pl.pallas_call(
         functools.partial(deliver_kernel, parts=tuple(len(group) for group in shares), heads=heads),
-        grid=(2,),
+        grid=(1,),
         in_specs=[pl.BlockSpec((block, features), lambda i: (i, 0)), vm] + [vm] * len(flat),
         out_specs=[pl.BlockSpec((block, features), lambda i: (i, 0))] + [vm] * (len(shares) + 6),
         out_shape=[jax.ShapeDtypeStruct(g_tokens.shape, F32)]

time: 230 us -> 230 us (level)
  no operation moved by 1% of the time
where the time goes in v3:
time: 230 us
  Pallas kernels  218 us (95%)
  matrix products  9.48 us (4%)
    pallas_call x1, Pallas kernels, attend_and_project_backward(): pl.pallas_call(functools.partial(back_kernel, n_ext=n_ext, units=units, t...  70.4 us
    pallas_call x1, Pallas kernels, mlp_backward(): pl.pallas_call(functools.partial(mlp_back_kernel, n_ext=len(views), units...  42.8 us
    pallas_call x1, Pallas kernels, attend_forward(): pl.pallas_call(functools.partial(fwd_kernel, rows=rows, pair_scale=pair_s...  37.8 us
    pallas_call x1, Pallas kernels, pair_head(): pl.pallas_call(functools.partial(pair_kernel, scale=scale), in_specs=[vm]...  31.1 us
    pallas_call x1, Pallas kernels, mlp_forward(): pl.pallas_call(mlp_forward_kernel, grid=(hidden // feats,), in_specs=[vm,...  21.9 us
    dot_general x1, matrix products, dot(): return lax.dot_general(a, b, dims, preferred_element_type=F32)  9.48 us
    pallas_call x1, Pallas kernels, project_forward(): pl.pallas_call(project_kernel, grid=(width // block,), in_specs=[pl.Block...  9.15 us

profile of v3, /device:TPU:0, one launch (start us, length us, event | category | flops | bytes accessed | tf_op | source)
XLA Modules:
  0.0 230.1 jit_solution(2281036777130668808)
XLA Ops:
  0.6 9.1 %project_forward.1 = (bf16[1024,768]{1,0:T(8,128)(2,1)}, bf16[1024,2304]{1,0:T(8,128)(2,1)}, f32[1024,128]{1,0:T(8,128)}) custom-call(bf16[1024,768]{1,0:T(8,128)(2,1)} %refs_11_.1, f32[768]{0:T(1024)} %refs_13_.1, f32[768]{0:T(1024)} %bias_ref.2, bf16[768,2304]{1,0:T(8,128)(2,1)} %refs_9_.3, s32[4,1024]{1,0:T(4,128)} %refs_7_.1, s32[2,512]{1,0:T(2,128)} %page_ref.1), custom_call_target="tpu_custom_call" | custom-call | tf_op jit(solution)/shard_map/project_forward/pallas_call | solution.py:614
  9.8 0.0 copy-start.8
  9.8 0.0 copy-start.9
  9.8 0.0 copy-start.10
  9.8 37.8 %attend_forward.1 = (bf16[1024,768]{1,0:T(8,128)(2,1)}, bf16[12,2,512,512]{3,2,1,0:T(8,128)(2,1)}, f32[1024,768]{1,0:T(8,128)}, bf16[4,128,512]{2,1,0:T(8,128)(2,1)}, bf16[4,128,512]{2,1,0:T(8,128)(2,1)}) custom-call(bf16[1024,2304]{1,0:T(8,128)(2,1)} %get-tuple-element.63.q_ref.k_ref.v_ref.refs_0_.refs_1_.refs_2_, ...), custom_call_target="tpu_custom_call" | custom-call | tf_op jit(solution)/shard_map/attend_forward/pallas_call | solution.py:170
  47.7 0.0 copy-done
  47.7 0.0 copy-done.7
  47.7 0.0 copy-done.8
  47.7 0.0 copy-done.9
  47.7 0.0 copy-done.10
  47.7 0.0 copy-start.1
  47.7 0.0 copy-start.5
  47.8 0.0 copy-start.6
  47.8 21.9 %mlp_forward.1 = (f32[1024,768]{1,0:T(8,128)}, bf16[1024,768]{1,0:T(8,128)(2,1)S(1)}, bf16[1024,3072]{1,0:T(8,128)(2,1)}, bf16[1024,3072]{1,0:T(8,128)(2,1)}, bf...) custom-call(bf16[1024,768]{1,0:T(8,128)(2,1)} %get-tuple-element.65.ctx_ref.refs_7_.refs_5_, ...), custom_call_target="tpu_custom_call" | custom-call | tf_op jit(solution)/shard_map/mlp_forward/pallas_call | solution.py:679
  69.7 1.2 copy-done.2
  70.9 0.0 copy-done.5
  70.9 31.1 %pair_head.1 = (f32[512,512]{1,0:T(8,128)S(1)}, bf16[768,768]{1,0:T(8,128)(2,1)}, bf16[768,768]{1,0:T(8,128)(2,1)}, f32[1024,768]{1,0:T(8,128)}, bf16[1024,768]{1,0:T(8,128)(2,1)}) custom-call(bf16[128,768]{1,0:T(8,128)(2,1)S(1)} %get-tuple-element.67.emb_ref, bf16[768,768]{1,0:T(8,128)(2,1)} %left_ref.1, bf16[768,768]{1,0:T(8,128)(2,1)} %right_ref.1, ...), custom_call_target="tpu_custom_call" | custom-call | tf_op jit(solution)/shard_map/pair_head/pallas_call | solution.py:883
  102.0 0.0 copy-start.3
  102.0 9.5 %convolution_convert_fusion = bf16[3072,768]{1,0:T(8,128)(2,1)} fusion(bf16[1024,3072]{1,0:T(8,128)(2,1)} %get-tuple-element.80, bf16[1024,768]{1,0:T(8,128)(2,1)} %get-tuple-element.74.refs_3_), kind=kOutput, calls=%fused_computation | convolution fusion | flops 4834197504 | bytes 12582912 | tf_op jit(solution)/shard_map/dot_general | solution.py:21
  111.5 42.8 %mlp_backward.1 = (bf16[768,3072]{1,0:T(8,128)(2,1)}, f32[1024,768]{1,0:T(8,128)}, bf16[768,768]{1,0:T(8,128)(2,1)}, bf16[1024,768]{1,0:T(8,128)(2,1)}, f32[64,1...) custom-call(bf16[1024,3072]{1,0:T(8,128)(2,1)} %get-tuple-element.73, ...), custom_call_target="tpu_custom_call" | custom-call | tf_op jit(solution)/shard_map/mlp_backward/pallas_call | solution.py:1053
  154.3 70.4 %attend_backward.1 = (f32[1024,768]{1,0:T(8,128)}, f32[64,128]{1,0:T(8,128)}, f32[24,768]{1,0:T(8,128)}, f32[24,768]{1,0:T(8,128)}, f32[96,768]{1,0:T(8,128)}, /...) custom-call(bf16[1024,2304]{1,0:T(8,128)(2,1)} %get-tuple-element.63.q_ref.k_ref.v_ref.refs_0_.refs_1_.refs_2_, ...), custom_call_target="tpu_custom_call" | custom-call | tf_op jit(solution)/shard_map/attend_backward/pallas_call | solution.py:1442
  224.7 0.0 copy-start.4
  224.7 4.4 %deliver.1 = (f32[1024,768]{1,0:T(8,128)}, f32[144,128]{1,0:T(8,128)}, f32[144,128]{1,0:T(8,128)}, f32[144,128]{1,0:T(8,128)}, f32[576,128]{1,0:T(8,128)}, /*ind...) custom-call(f32[1024,768]{1,0:T(8,128)} %get-tuple-element.90.gx_ref, ...), custom_call_target="tpu_custom_call" | custom-call | tf_op jit(solution)/shard_map/deliver/pallas_call | solution.py:1110
  229.1 1.0 copy.35
  (7 shorter events, 0.0 us)
Async XLA Ops:
  9.8 37.9 %copy-start = (bf16[768,768]{1,0:T(8,128)(2,1)S(1)}, bf16[768,768]{1,0:T(8,128)(2,1)}, u32[]{:S(2)}) copy-start(bf16[768,768]{1,0:T(8,128)(2,1)} %refs_8_.1) | copy-start | bytes 3538948
  9.8 37.9 %copy-start.7 = (f32[768]{0:T(1024)S(1)}, f32[768]{0:T(1024)}, u32[]{:S(2)}) copy-start(f32[768]{0:T(1024)} %refs_9_.2) | copy-start | bytes 9220
  9.8 37.9 %copy-start.8 = (s32[2,512]{1,0:T(2,128)S(1)}, s32[2,512]{1,0:T(2,128)}, u32[]{:S(2)}) copy-start(s32[2,512]{1,0:T(2,128)} %seg_ref.3) | copy-start | bytes 12292
  9.8 37.9 %copy-start.9 = (f32[3072]{0:T(1024)S(1)}, f32[3072]{0:T(1024)}, u32[]{:S(2)}) copy-start(f32[3072]{0:T(1024)} %param.31) | copy-start | bytes 36868
  9.8 37.9 %copy-start.10 = (f32[768]{0:T(1024)S(1)}, f32[768]{0:T(1024)}, u32[]{:S(2)}) copy-start(f32[768]{0:T(1024)} %bias_ref.3) | copy-start | bytes 9220
  47.7 23.1 %copy-start.1 = (s32[1,512,512]{2,1,0:T(8,128)S(1)}, s32[1,512,512]{2,1,0:T(8,128)}, u32[]{:S(2)}) copy-start(s32[1,512,512]{2,1,0:T(8,128)} %param.23) | copy-start | bytes 3145732
  47.7 23.1 %copy-start.5 = (bf16[4,128,512]{2,1,0:T(8,128)(2,1)S(1)}, bf16[4,128,512]{2,1,0:T(8,128)(2,1)}, u32[]{:S(2)}) copy-start(bf16[4,128,512]{2,1,0:T(8,128)(2,1)} %get-tuple-element.68.rowp_ref) | copy-start | bytes 1572868
  47.8 23.1 %copy-start.6 = (bf16[4,128,512]{2,1,0:T(8,128)(2,1)S(1)}, bf16[4,128,512]{2,1,0:T(8,128)(2,1)}, u32[]{:S(2)}) copy-start(bf16[4,128,512]{2,1,0:T(8,128)(2,1)} %get-tuple-element.69.colp_ref) | copy-start | bytes 1572868
  69.7 1.2 copy-start.2
  102.0 9.5 %copy-start.3 = (f32[512,512]{1,0:T(8,128)}, f32[512,512]{1,0:T(8,128)S(1)}, u32[]{:S(2)}) copy-start(f32[512,512]{1,0:T(8,128)S(1)} %get-tuple-element.70) | copy-start | bytes 3145732
  224.7 4.4 %copy-start.4 = (f32[512,512]{1,0:T(8,128)S(1)}, f32[512,512]{1,0:T(8,128)}, u32[]{:S(2)}) copy-start(f32[512,512]{1,0:T(8,128)} %copy-done.3) | copy-start | bytes 3145732
